TPU v7x, 256 devices: a whole 4x4x8 slice. The times are simulated.
256 devices in a mesh: seq: 64 (over x, z, core), tp: 4 (over y).
Axes of the slice: x: 4, y: 4, z: 8, core: 2. Of those that a mesh axis runs over, the one named last changes fastest.
Arguments:
- tokens: bfloat16 [4096, 2048], P('seq'), may hold values from -6 to 6
- qkv_weight: bfloat16 [2048, 3, 2048], P('seq', None, 'tp'), may hold values from -0.125 to 0.125
- out_weight: bfloat16 [2048, 2048], P('tp', 'seq'), may hold values from -0.125 to 0.125
- kv_cache: bfloat16 [64, 8, 64, 2, 2048], P(None, None, 'seq', None, 'tp')
- lengths: int32 [64], replicated, may hold values from 64 to 448, as said below
- parents: int32 [64, 64], replicated, may hold values from -1 to 62, as said below
- leaves: int32 [64], replicated, may hold values from 32 to 63
- deal: int32 [64], replicated, may hold values from 0 to 63, each once
Outputs:
- branch_out: bfloat16 [4096, 2048], P('seq', 'tp')
- new_cache: bfloat16 [64, 8, 64, 2, 2048], P(None, None, 'seq', None, 'tp')
Inputs may be any that keep to these rules, and one draw needn't show every extreme that they name: `lengths`: every length is at least 64, and at most 448, both reached. parents[r, 0] = -1 and 0 <= parents[r, j] < j for j > 0.
All inputs are finite; a program needn't handle non-finite values.
Results may differ from a plain program's by a relative error of at most 0.012.
The roundings to bfloat16 on the way count: a program that leaves them out, or rounds other values in their place, can miss the bound.
Values may be sent and summed in bfloat16 or wider, within the bound.
A program may use at most 64 MiB of HBM per device.

v0:
```python
import jax
import jax.numpy as jnp
from jax import lax
from jax.sharding import PartitionSpec as P

HD = 128
SINKS = 4


def ancestry(parent_row):
    size = parent_row.shape[0]
    ids = jnp.arange(size, dtype=jnp.int32)
    links = (parent_row[:, None] == ids[None, :]).astype(jnp.float32)
    reach = jnp.eye(size, dtype=jnp.float32) + links
    for turn in range((size - 1).bit_length()):
        reach = jnp.minimum(jnp.dot(reach, reach, precision=lax.Precision.HIGHEST), 1.0)
    return reach


def rotate(values, places):
    width = values.shape[-1]
    half = width // 2
    frequency = 10000.0 ** (-2.0 * jnp.arange(half, dtype=jnp.float32) / width)
    angle = places.astype(jnp.float32)[:, None] * frequency[None, :]
    cosine = jnp.cos(angle)[:, None, :]
    sine_part = jnp.sin(angle)[:, None, :]
    lower_half = values[..., :half]
    upper_half = values[..., half:]
    return jnp.concatenate(
        [
            lower_half * cosine - upper_half * sine_part,
            upper_half * cosine + lower_half * sine_part,
        ],
        axis=-1,
    )


def on_device(tokens, qkv_weight, out_weight, kv_cache, lengths, parents, leaves, deal):
    shard_count = lax.axis_size("seq")
    own_index = lax.axis_index("seq")
    rows = tokens.shape[0]
    width_local = out_weight.shape[0]
    heads_local = width_local // HD
    requests = deal.shape[0]
    positions_local = kv_cache.shape[1]
    capacity = positions_local * shard_count
    window = capacity // 2
    scale = float(HD) ** (-0.5)
    wide = tokens.astype(jnp.float32)
    centred = wide - jnp.mean(wide, axis=-1, keepdims=True)
    normed = (
        centred * lax.rsqrt(jnp.mean(centred * centred, axis=-1, keepdims=True) + 1e-05)
    ).astype(jnp.bfloat16)
    piece = lax.all_gather(qkv_weight, "seq", axis=0, tiled=True)
    columns = normed
    projected = jnp.dot(
        columns, piece.reshape(piece.shape[0], 3 * width_local), preferred_element_type=jnp.float32
    )
    projected = projected.reshape(rows, 3, heads_local, HD)
    request = deal[own_index]
    length = lengths[request]
    reach = ancestry(parents[request])
    depth = (jnp.sum(reach, axis=1) - 1.0).astype(jnp.int32)
    places = length + depth
    query = rotate(projected[:, 0], places).astype(jnp.bfloat16)
    key_new = rotate(projected[:, 1], places).astype(jnp.bfloat16)
    value_new = projected[:, 2].astype(jnp.bfloat16)
    by_slot = kv_cache[deal]
    every_query = lax.all_gather(query.reshape(rows, width_local), "seq", axis=0, tiled=True)
    slot_queries = every_query.reshape(requests, rows, heads_local, HD)
    blocks = by_slot.reshape(requests, positions_local, 2, heads_local, HD)
    scores = (
        jnp.einsum(
            "rqhd,rchd->rqhc", slot_queries, blocks[:, :, 0], preferred_element_type=jnp.float32
        )
        * scale
    )
    location = jnp.arange(positions_local, dtype=jnp.int32) * shard_count + own_index
    slot_length = lengths[deal][:, None]
    valid = (location[None, :] < slot_length) & (
        (location[None, :] < SINKS) | (location[None, :] >= slot_length - window)
    )
    valid_full = valid[:, None, None, :]
    masked = jnp.where(valid_full, scores, -1e30)
    cache_peak = lax.pmax(jnp.max(masked, axis=-1), "seq")
    weights = jnp.where(valid_full, jnp.exp(masked - cache_peak[..., None]), 0.0)
    weighted_all = jnp.einsum(
        "rqhc,rchd->rqhd",
        weights.astype(jnp.bfloat16),
        blocks[:, :, 1],
        preferred_element_type=jnp.float32,
    )
    totals_all = jnp.sum(weights, axis=-1)
    weighted, cache_total = (
        lax.psum_scatter(
            weighted_all.reshape(requests * rows, width_local),
            "seq",
            scatter_dimension=0,
            tiled=True,
        ),
        lax.psum_scatter(
            totals_all.reshape(requests * rows, heads_local), "seq", scatter_dimension=0, tiled=True
        ),
    )
    weighted = weighted.reshape(rows, heads_local, HD)
    cache_top = lax.dynamic_slice_in_dim(cache_peak, own_index, 1, 0)[0]
    tree_scores = (
        jnp.einsum("qhd,khd->qhk", query, key_new, preferred_element_type=jnp.float32) * scale
    )
    tree_valid = (reach > 0.5)[:, None, :]
    tree_masked = jnp.where(tree_valid, tree_scores, -1e30)
    joint = jnp.maximum(cache_top, jnp.max(tree_masked, axis=-1))
    tree_weights = jnp.where(tree_valid, jnp.exp(tree_masked - joint[..., None]), 0.0)
    ratio = jnp.exp(cache_top - joint)
    tree_sum = jnp.einsum(
        "qhk,khd->qhd",
        tree_weights.astype(jnp.bfloat16),
        value_new,
        preferred_element_type=jnp.float32,
    )
    attended = (weighted * ratio[..., None] + tree_sum) / (
        cache_total * ratio + jnp.sum(tree_weights, axis=-1)
    )[..., None]
    attended = attended.astype(jnp.bfloat16).reshape(rows, width_local)
    columns = jnp.dot(
        attended,
        lax.all_gather(out_weight, "seq", axis=1, tiled=True),
        preferred_element_type=jnp.float32,
    )
    branch_out = lax.psum_scatter(
        columns.astype(jnp.bfloat16), "tp", scatter_dimension=1, tiled=True
    )
    on_path = reach[leaves[request]]
    path_end = (jnp.sum(on_path) - 1.0).astype(jnp.int32)
    levels = jnp.arange(rows, dtype=jnp.int32)
    picker = on_path[None, :] * (depth[None, :] == levels[:, None]).astype(jnp.float32)
    fresh = jnp.stack(
        [key_new.reshape(rows, width_local), value_new.reshape(rows, width_local)], axis=1
    ).reshape(rows, 2 * width_local)
    path_rows = jnp.dot(
        picker.astype(jnp.bfloat16), fresh, preferred_element_type=jnp.float32
    ).astype(jnp.bfloat16)
    slots = (rows + shard_count - 1) // shard_count
    target = jnp.arange(shard_count, dtype=jnp.int32)[:, None]
    slot_ids = jnp.arange(slots, dtype=jnp.int32)[None, :]
    offset = (target - length) % shard_count + slot_ids * shard_count
    flags = offset <= path_end
    outgoing = jnp.where(
        flags[..., None], path_rows[jnp.clip(offset, 0, rows - 1)], jnp.zeros((), jnp.bfloat16)
    )
    arrived, arrived_flags = (
        lax.all_to_all(outgoing, "seq", split_axis=0, concat_axis=0, tiled=True),
        lax.all_to_all(flags.astype(jnp.bfloat16), "seq", split_axis=0, concat_axis=0, tiled=True),
    )
    source_length = lengths[deal][:, None]
    offset_in = (own_index - source_length) % shard_count + slot_ids * shard_count
    local_slot = (source_length + offset_in) // shard_count
    target_slot = jnp.where(arrived_flags > 0.5, local_slot, positions_local)
    request_rows = deal[:, None]
    flat = kv_cache.reshape(requests, positions_local, 2 * width_local)
    updated = flat.at[request_rows, target_slot].set(arrived, mode="drop")
    return (branch_out, updated.reshape(kv_cache.shape))


def solution(mesh):
    placed = (
        P("seq", None),
        P("seq", None, "tp"),
        P("tp", "seq"),
        P(None, None, "seq", None, "tp"),
        P(),
        P(),
        P(),
        P(),
    )
    return jax.shard_map(
        on_device,
        mesh=mesh,
        in_specs=placed,
        out_specs=(P("seq", "tp"), P(None, None, "seq", None, "tp")),
        check_vma=False,
    )
```

profile of v0, /device:TPU:1, one launch (start us, length us, event | category | flops | bytes accessed | tf_op | source)
XLA Modules:
  0.0 782.7 jit_solution(12361154958030504508)
XLA Ops:
  7.2 0.7 all-gather.4.cloned.1.call-update
  8.0 1.2 dynamic_slice.18
  11.2 1.3 dynamic_slice.19
  12.5 1.1 convert_reduce_fusion
  13.6 1.2 fusion.21
  15.7 0.3 fusion.67
  16.0 0.7 add_convert_fusion
  16.9 78.6 %all-gather.4.cloned.1.call-done = bf16[2048,3,512]{2,0,1:T(8,128)(2,1)} async-done(((bf16[32,3,512]{2,0,1:T(8,128)(2,1)}), bf16[2048,3,512]{2,0,1:T(8,128)(2,1)}) %all-gather.4.cloned.1.call-update) | async-done | bytes 6291472 | tf_op jit(solution)/shard_map/all_gather | solution.py:54
  95.5 8.8 %copy.79 = bf16[2048,3,512]{0,2,1:T(8,128)(2,1)} copy(bf16[2048,3,512]{2,0,1:T(8,128)(2,1)} %all-gather.4.cloned.1.call-done) | data formatting | bytes 12582912 | tf_op jit(solution)/shard_map/all_gather | solution.py:54
  104.4 4.9 fusion.28
  109.6 0.6 copy_bitcast_fusion.7
  110.4 0.8 gather_fusion.1
  111.4 2.7 gather_fusion
  114.0 0.7 reshape.509
  114.7 1.4 fusion.66
  116.1 70.0 %all-gather.6.cloned.1.call-done = bf16[4096,512]{1,0:T(8,128)(2,1)} async-done(((bf16[64,512]{1,0:T(8,128)(2,1)}), bf16[4096,512]{1,0:T(8,128)(2,1)}) %all-gather.6.cloned.1.call-update) | async-done | bytes 4194320 | tf_op jit(solution)/shard_map/all_gather | solution.py:69
  186.1 6.9 reshape.463
  193.0 5.2 fusion.68
  198.3 173.5 %all-reduce.2.cloned.1.call-done = f32[64,64,4]{1,2,0:T(4,128)} async-done(((f32[64,64,4]{1,2,0:T(4,128)}), f32[64,64,4]{1,2,0:T(4,128)}) %all-reduce.2.cloned.1.call-update) | async-done | bytes 65552 | tf_op jit(solution)/shard_map/pmax | solution.py:85
  371.8 1.5 fusion.17
  373.3 2.0 copy.101
  375.6 5.0 convolution_bitcast_fusion
  380.6 14.6 %copy.82 = f32[64,64,4,128]{3,2,1,0:T(4,128)} copy(f32[64,64,4,128]{3,1,2,0:T(8,128)} %convolution_bitcast_fusion) | data formatting | bytes 16777216 | tf_op jit(solution)/shard_map/rqhc,rchd->rqhd/transpose | solution.py:87
  395.2 7.7 copy.137
  402.9 0.5 all-gather.8.cloned.1.call-update
  403.5 0.6 dynamic_slice.22
  406.0 0.6 fusion.60
  407.3 0.6 compare_convert_fusion
  407.9 0.7 copy.88
  408.6 6.5 all-to-all-start
  415.2 0.7 fusion.57
  415.9 0.6 fusion.53
  416.6 0.8 reshape.468
  417.4 7.0 all-to-all-done
  424.8 0.7 gather_fusion.2
  425.8 83.3 %reduce-scatter.10.cloned.1.call-done = f32[64,4]{1,0:T(8,128)} async-done(((f32[4096,4]{1,0:T(8,128)}), f32[64,4]{1,0:T(8,128)}) %reduce-scatter.10.cloned.1.call-update) | async-done | bytes 1040
  509.1 0.8 copy.100
  509.9 154.3 %reduce-scatter.6.cloned.1.call-done = f32[64,512]{1,0:T(8,128)} async-done(((f32[4096,512]{1,0:T(8,128)}), f32[64,512]{1,0:T(8,128)}) %reduce-scatter.6.cloned.1.call-update) | async-done | bytes 131088 | tf_op jit(solution)/shard_map/reduce_scatter | solution.py:95
  664.2 1.1 fusion.16
  665.3 82.3 %all-gather.8.cloned.1.call-done = bf16[512,2048]{0,1:T(8,128)(2,1)} async-done(((bf16[512,32]{0,1:T(8,128)(2,1)}), bf16[512,2048]{0,1:T(8,128)(2,1)}) %all-gather.8.cloned.1.call-update) | async-done | bytes 2097168 | tf_op jit(solution)/shard_map/all_gather | solution.py:127
  747.6 3.0 convolution_convert_fusion
  750.7 0.5 broadcast.566
  751.2 0.7 reduce.1
  751.9 0.7 reshape.512
  752.6 6.6 all-to-all-start.1
  759.3 10.3 %all-to-all-done.1 = bf16[64,2,512]{2,1,0:T(2,128)(2,1)S(1)} async-done(((bf16[64,2,512]{2,1,0:T(2,128)(2,1)}), bf16[64,2,512]{2,1,0:T(2,128)(2,1)S(1)}, u32[]{:S(2)}, u32[]{:S(2)}) %all-to-all-start.1) | async-done | bytes 131104 | tf_op jit(solution)/shard_map/all_to_all | solution.py:152
  769.8 4.5 scatter_fusion
  774.2 1.6 reshape.470
  (77 shorter events, 3.3 us)
Async XLA Ops:
  7.2 5.3 copy-start
  7.2 88.3 %all-gather.4.cloned.1.call-start = ((), (), s32[]{:S(2)}) async-start(), calls=%async_computation.5 | async-start | bytes 6389760 | tf_op jit(solution)/shard_map/all_gather | solution.py:54
  7.9 178.2 %all-gather.6.cloned.1.call-start = ((), (), s32[]{:S(2)}) async-start(), calls=%async_computation.6 | async-start | bytes 4259840 | tf_op jit(solution)/shard_map/all_gather | solution.py:69
  16.9 87.5 %copy-start.3 = (bf16[64,2048]{1,0:T(8,128)(2,1)S(1)}, bf16[64,2048]{1,0:T(8,128)(2,1)}, u32[]{:S(2)}) copy-start(bf16[64,2048]{1,0:T(8,128)(2,1)} %param.8) | copy-start | bytes 786436
  104.4 6.0 copy-start.9
  104.4 6.0 copy-start.1
  104.4 7.0 copy-start.2
  109.3 2.1 copy-start.6
  110.3 261.5 %all-reduce.2.cloned.1.call-start = ((), (), s32[]{:S(2)}) async-start(), calls=%async_computation.7 | async-start | bytes 262144 | tf_op jit(solution)/shard_map/pmax | solution.py:85
  116.1 76.9 %copy-start.5 = (bf16[64,8,1,4,128]{4,3,2,1,0:T(4,128)(2,1)S(1)}, bf16[64,8,1,4,128]{4,3,2,1,0:T(4,128)(2,1)}, u32[]{:S(2)}) copy-start(bf16[64,8,1,4,128]{4,3,2,1,0:T(4,128)(2,1)} %get-tuple-element.5) | copy-start | bytes 1572868
  198.2 177.4 %copy-start.4 = (bf16[64,8,1,4,128]{4,3,2,1,0:T(4,128)(2,1)S(1)}, bf16[64,8,1,4,128]{4,3,2,1,0:T(4,128)(2,1)}, u32[]{:S(2)}) copy-start(bf16[64,8,1,4,128]{4,3,2,1,0:T(4,128)(2,1)} %get-tuple-element.4) | copy-start | bytes 1572868
  198.2 310.9 %reduce-scatter.10.cloned.1.call-start = ((), (), s32[]{:S(2)}) async-start(), calls=%async_computation.11 | async-start | bytes 2129920
  371.8 3.8 copy-start.8
  375.3 288.8 %reduce-scatter.6.cloned.1.call-start = ((), (), s32[]{:S(2)}) async-start(), calls=%async_computation.8 | async-start | bytes 8519680 | tf_op jit(solution)/shard_map/reduce_scatter | solution.py:95
  402.8 0.7 copy-start.10
  402.8 21.8 %copy-start.7 = (f32[64,3,4,128]{3,0,2,1:T(8,128)S(1)}, f32[64,3,4,128]{3,0,2,1:T(8,128)}, u32[]{:S(2)}) copy-start(f32[64,3,4,128]{3,0,2,1:T(8,128)} %copy-done.6) | copy-start | bytes 1179652
  402.8 344.7 %all-gather.8.cloned.1.call-start = ((), (), s32[]{:S(2)}) async-start(), calls=%async_computation.9 | async-start | bytes 2129920 | tf_op jit(solution)/shard_map/all_gather | solution.py:127
  408.6 15.7 %all-to-all-start = ((bf16[64,1,1]{2,1,0:T(2,128)(2,1)}), bf16[64,1,1]{2,1,0:T(2,128)(2,1)S(1)}, u32[]{:S(2)}, u32[]{:S(2)}) async-start(bf16[64,1,1]{2,1,0:T(2,128)(2,1)} %copy.88), calls=%async_computation.2 | async-start | bytes 65536 | tf_op jit(solution)/shard_map/all_to_all | solution.py:153
  415.1 360.7 %reduce-scatter.8.cloned.1.call-start = ((), (), s32[]{:S(2)}) async-start(), calls=%async_computation.10 | async-start | bytes 327680 | tf_op jit(solution)/shard_map/reduce_scatter | solution.py:130
  752.6 17.0 %all-to-all-start.1 = ((bf16[64,2,512]{2,1,0:T(2,128)(2,1)}), bf16[64,2,512]{2,1,0:T(2,128)(2,1)S(1)}, u32[]{:S(2)}, u32[]{:S(2)}) async-start(bf16[64,2,512]{2,1,0:T(2,128)(2,1)} %reshape.512), calls=%async_computation.3 | async-start | bytes 262144 | tf_op jit(solution)/shard_map/all_to_all | solution.py:152
Sparse Core Ops, SparseCore 0:
  10.8 84.6 all-gather.3
  110.4 75.7 all-gather.5
  198.3 173.4 all-reduce.1
  375.7 133.3 reduce-scatter.9
  513.1 150.9 reduce-scatter.5
  666.8 80.7 all-gather.7
  750.8 18.7 reduce-scatter.7
where the time goes:
time: 784 us; the launch traced here: 783 us
  waiting for transfers between devices  661 us (84%)
  local copies, waits for them, and re-layouts  60.3 us (8%)
  matrix products  20.7 us (3%)
  between operations  19.1 us (2%)
  starting transfers between devices  13.6 us (2%)
  other arithmetic  8.42 us (1%)
    pmax x1, waiting for transfers between devices, on_device(): cache_peak = lax.pmax(jnp.max(masked, axis=-1), 'seq')  174 us
    reduce_scatter x1, waiting for transfers between devices, on_device(): lax.psum_scatter(weighted_all.reshape(requests * rows, width_local), 'seq...  154 us
    unnamed x8, waiting for transfers between devices  84.6 us
    all_gather x1, waiting for transfers between devices, on_device(): lax.all_gather(out_weight, 'seq', axis=1, tiled=True)  82.3 us
    all_gather x1, waiting for transfers between devices, on_device(): piece = lax.all_gather(qkv_weight, 'seq', axis=0, tiled=True)  78.6 us
    all_gather x1, waiting for transfers between devices, on_device(): lax.all_gather(query.reshape(rows, width_local), 'seq', axis=0, tiled=True)  70 us
  transfers between devices with their start and end apart: 9, of which 8 were waited for; matrix products, arithmetic and copies ran while one was open for 7% of the time, Pallas kernels for 0%

commit v1 on v0

v1 whole, which is shorter than its diff:
```python
import functools

import jax
import jax.numpy as jnp
from jax import lax
from jax.experimental import pallas as pl
from jax.experimental.pallas import tpu as pltpu
from jax.sharding import PartitionSpec as P

HD = 128
SINKS = 4
X, Z, CORES = 4, 8, 2
SEQ = X * Z * CORES
TP = 4
ROWS = 64
SLOTS = 4
WIDTH = 512
HEADS = WIDTH // HD
WINDOW = 256
DEEP = 2048


def nt(a, b):
    return lax.dot_general(
        a, b, (((1,), (1,)), ((), ())), preferred_element_type=jnp.float32
    )


def nn(a, b):
    return lax.dot_general(
        a, b, (((1,), (0,)), ((), ())), preferred_element_type=jnp.float32
    )


def pre_kernel(
    deal, lengths, leaves, tokens, parents, freq, cache,
    packed, sinks, normed, reach_out, cos_out, sin_out, pick_out, depth_out,
    par_pad,
):
    me = lax.axis_index("seq")

    def pack(t, carry):
        r = deal[t]
        base = jnp.maximum(lengths[r] - WINDOW, 0)
        first = lax.shift_right_logical(base - me + (SEQ - 1), 6)
        packed[t] = cache[r, pl.ds(first, SLOTS)]
        sinks[t] = cache[r, 0]
        return carry

    lax.fori_loop(0, ROWS, pack, 0)

    wide = tokens[...].astype(jnp.float32)
    centred = wide - jnp.mean(wide, axis=-1, keepdims=True)
    scale = lax.rsqrt(jnp.mean(centred * centred, axis=-1, keepdims=True) + 1e-05)
    normed[...] = (centred * scale).astype(jnp.bfloat16)

    request = deal[me]
    length = lengths[request]
    leaf = leaves[request]
    sub = lax.broadcasted_iota(jnp.int32, (ROWS, ROWS), 0)
    lane = lax.broadcasted_iota(jnp.int32, (ROWS, ROWS), 1)
    eye = jnp.where(sub == lane, 1.0, 0.0)
    row = parents[pl.ds(request, 1), :]
    up = eye + jnp.where(row == sub, 1.0, 0.0)
    for _ in range(6):
        half = up.astype(jnp.bfloat16)
        up = jnp.minimum(nn(half, half), 1.0)
    reach = nt(eye.astype(jnp.bfloat16), up.astype(jnp.bfloat16))
    reach_out[...] = reach
    depth_row = (jnp.sum(up, axis=0, keepdims=True) - 1.0).astype(jnp.int32)
    depth_col = (jnp.sum(reach, axis=1, keepdims=True) - 1.0).astype(jnp.int32)
    places = (length + depth_col).astype(jnp.float32)
    angle = places * freq[...]
    cos_out[...] = jnp.cos(angle)
    wave = jnp.sin(angle)
    wide_lane = lax.broadcasted_iota(jnp.int32, (ROWS, HD), 1)
    sin_out[...] = jnp.where(wide_lane < HD // 2, -wave, wave)
    on_path = jnp.sum(jnp.where(sub == leaf, reach, 0.0), axis=0, keepdims=True)
    offset = lax.rem(sub - length + 8 * SEQ, SEQ)
    hit = (on_path > 0.5) & (depth_row == offset)
    pick_out[...] = jnp.where(hit, 1.0, 0.0).astype(jnp.bfloat16)

    lanes = lax.broadcasted_iota(jnp.int32, (ROWS, HD), 1)
    par_pad[...] = lanes
    par_pad[:, 0:ROWS] = parents[...]
    par = par_pad[...]
    climb = jnp.where((lanes < ROWS) & (par >= 0), 1, 0)
    jump = jnp.where(par < 0, 0, par)
    for _ in range(6):
        climb = climb + jnp.take_along_axis(climb, jump, axis=1)
        jump = jnp.take_along_axis(jump, jump, axis=1)
    depth_out[...] = climb


def comm_kernel(
    wq, wo, kv, sk, WQ, WO, KV, SK,
    own_sem, ra, rb, sa, sb, sib_sa, sib_sb, sib_ra, sib_rb,
    kv_s, kv_r, sk_s, sk_r,
):
    me = lax.axis_index("seq")
    x = me // (Z * CORES)
    z = lax.rem(me // CORES, Z)
    c = lax.rem(me, CORES)

    def idx(dx, dz):
        return (
            lax.rem(x + (dx + X), X) * Z + lax.rem(z + (dz + Z), Z)
        ) * CORES + c

    sibling = me + 1 - 2 * c
    to = {
        "x+": {"seq": idx(1, 0)},
        "x-": {"seq": idx(-1, 0)},
        "z+": {"seq": idx(0, 1)},
        "z-": {"seq": idx(0, -1)},
        "s": {"seq": sibling},
    }
    shift = {"x+": (-1, 0), "x-": (1, 0), "z+": (0, -1), "z-": (0, 1)}

    barrier = pltpu.get_barrier_semaphore()

    def greet(k, carry):
        pl.semaphore_signal(barrier, 1, device_id={"seq": lax.rem(me + k, SEQ)})
        return carry

    lax.fori_loop(1, SEQ, greet, 0)
    pl.semaphore_wait(barrier, SEQ - 1)

    def send_a(dx, dz, way):
        at = idx(dx, dz)
        src = wq if (dx, dz) == (0, 0) else WQ.at[:, at]
        if way == "s":
            send, recv = sib_sa, sib_ra
        else:
            ox, oz = shift[way]
            send, recv = sa, ra.at[(dx + ox) % X, (dz + oz) % Z]
        pltpu.make_async_remote_copy(
            src_ref=src, dst_ref=WQ.at[:, at], send_sem=send, recv_sem=recv,
            device_id=to[way],
        ).start()

    def send_b(dx, dz, way):
        at = idx(dx, dz)
        src = wo if (dx, dz) == (0, 0) else WO.at[at]
        if way == "s":
            send, recv = sib_sb, sib_rb
        else:
            ox, oz = shift[way]
            send, recv = sb, rb.at[(dx + ox) % X, (dz + oz) % Z]
        pltpu.make_async_remote_copy(
            src_ref=src, dst_ref=WO.at[at], send_sem=send, recv_sem=recv,
            device_id=to[way],
        ).start()

    def wait_a(dx, dz):
        at = idx(dx, dz)
        pltpu.make_async_copy(
            WQ.at[:, at], WQ.at[:, at], ra.at[dx % X, dz % Z]
        ).wait()

    def wait_b(dx, dz):
        at = idx(dx, dz)
        pltpu.make_async_copy(WO.at[at], WO.at[at], rb.at[dx % X, dz % Z]).wait()

    def route_a(dx, dz):
        out = []
        if dx == 0:
            if dz == 0:
                out += ["z+", "z-"]
            elif -4 < dz < 0:
                out += ["z+"]
            elif 0 < dz < 3:
                out += ["z-"]
            out += ["x+", "x-"]
        elif dx == -1 and dz % 2 == 0:
            out += ["x+"]
        elif dx == 1 and dz % 2 == 1:
            out += ["x-"]
        return out + ["s"]

    def route_b(dx, dz):
        out = []
        if dz == 0:
            if dx == 0:
                out += ["x+", "x-"]
            elif dx == -1:
                out += ["x+"]
            out += ["z+", "z-"]
        else:
            far = 4 if dx % 2 == 0 else 3
            if -far < dz < 0:
                out += ["z+"]
            elif 0 < dz < 7 - far:
                out += ["z-"]
        return out + ["s"]

    own_a = pltpu.make_async_copy(wq, WQ.at[:, me], own_sem.at[0])
    own_b = pltpu.make_async_copy(wo, WO.at[me], own_sem.at[1])
    own_kv = pltpu.make_async_copy(kv.at[me], KV.at[me], own_sem.at[2])
    for way in route_a(0, 0):
        send_a(0, 0, way)
    for way in route_b(0, 0):
        send_b(0, 0, way)
    own_a.start()
    own_b.start()
    own_kv.start()

    def scatter(k, carry):
        t = lax.rem(me + k, SEQ)
        pltpu.make_async_remote_copy(
            src_ref=kv.at[t], dst_ref=KV.at[me], send_sem=kv_s, recv_sem=kv_r,
            device_id={"seq": t},
        ).start()
        return carry

    lax.fori_loop(1, SEQ, scatter, 0)

    @pl.when(me < SINKS)
    def _():
        pltpu.make_async_copy(sk.at[me], SK.at[me], sk_r).start()

        def spread(k, carry):
            t = lax.rem(me + k, SEQ)
            pltpu.make_async_remote_copy(
                src_ref=sk.at[t], dst_ref=SK.at[me], send_sem=sk_s, recv_sem=sk_r,
                device_id={"seq": t},
            ).start()
            return carry

        lax.fori_loop(1, SEQ, spread, 0)

    steps = []
    for dz in (-1, 1, -2, 2, -3, 3, -4):
        steps.append((2 * abs(dz), "a", 0, dz))
    for dx, cost in ((-1, 1), (1, 1), (-2, 2)):
        steps.append((2 * cost + 0.2, "b", dx, 0))
    for dz in (0, -1, 1, -2, 2, -3, 3, -4):
        for dx, cost in ((-1, 1), (1, 1), (-2, 2)):
            steps.append((2 * abs(dz) + 2 * cost + 0.5, "a", dx, dz))
    for dx in (0, -1, 1, -2):
        far = 4 if dx % 2 == 0 else 3
        for dz in list(range(-far, 0)) + list(range(1, 8 - far)):
            steps.append((2 * abs(dx) + 2 * abs(dz) + 0.6, "b", dx, dz))
    for _, kind, dx, dz in sorted(steps, key=lambda s: s[0]):
        if kind == "a":
            wait_a(dx, dz)
            for way in route_a(dx, dz):
                send_a(dx, dz, way)
        else:
            wait_b(dx, dz)
            for way in route_b(dx, dz):
                send_b(dx, dz, way)

    own_a.wait()
    own_b.wait()
    own_kv.wait()

    def all_of(ref, sem):
        pltpu.make_async_copy(ref, ref, sem).wait()

    others = pl.ds(0, SEQ - 1)
    pieces = SEQ // CORES
    all_of(KV.at[others], kv_r)
    all_of(SK, sk_r)
    all_of(WQ.at[:, pl.ds(0, pieces)], sib_ra)
    all_of(WO.at[pl.ds(0, pieces)], sib_rb)
    all_of(WQ.at[:, pl.ds(0, pieces - 1)], sa)
    all_of(WO.at[pl.ds(0, pieces - 1)], sb)
    all_of(WQ.at[:, pl.ds(0, pieces)], sib_sa)
    all_of(WO.at[pl.ds(0, pieces)], sib_sb)
    all_of(kv.at[others], kv_s)

    @pl.when(me < SINKS)
    def _():
        all_of(sk.at[others], sk_s)


def main_kernel(
    deal, lengths, normed, wq, wo, kv, sk, reach, cos, sin, pick,
    part, fresh_k, fresh_v, acc, att,
):
    step = pl.program_id(0)

    @pl.when(step == 0)
    def _():
        acc[...] = jnp.zeros_like(acc)

    for kind in range(3):
        acc[kind] += nn(normed[...], wq[kind])

    @pl.when(step == pl.num_programs(0) - 1)
    def _():
        length = lengths[deal[lax.axis_index("seq")]]
        scale = float(HD) ** (-0.5)
        base = jnp.maximum(length - WINDOW, 0)
        lane = lax.broadcasted_iota(jnp.int32, (ROWS, SEQ * SLOTS * 2), 1)
        shard = lax.shift_right_logical(lane, 3)
        slot = lax.shift_right_logical(lane & 7, 1)
        first = lax.shift_right_logical(base - shard + (SEQ - 1), 6)
        place = (first + slot) * SEQ + shard
        valid = (
            ((lane & 1) == 0)
            & (place < length)
            & ((place < SINKS) | (place >= length - WINDOW))
        )
        lane_s = lax.broadcasted_iota(jnp.int32, (ROWS, 2 * SINKS), 1)
        valid_s = ((lane_s & 1) == 0) & (
            length - WINDOW > lax.shift_right_logical(lane_s, 1)
        )
        tree = reach[...] > 0.5
        cosine = cos[...]
        sine = sin[...]

        def turn(v):
            return v * cosine + pltpu.roll(v, HD // 2, 1) * sine

        for h in range(HEADS):
            cols = slice(h * HD, (h + 1) * HD)
            q = turn(acc[0, :, cols]).astype(jnp.bfloat16)
            k = turn(acc[1, :, cols]).astype(jnp.bfloat16)
            v = acc[2, :, cols].astype(jnp.bfloat16)
            old = kv[:, cols]
            old_s = sk[:, cols]
            s = jnp.where(valid, nt(q, old) * scale, -1e30)
            s_s = jnp.where(valid_s, nt(q, old_s) * scale, -1e30)
            top = jnp.maximum(
                jnp.max(s, axis=-1, keepdims=True), jnp.max(s_s, axis=-1, keepdims=True)
            )
            w = jnp.where(valid, jnp.exp(s - top), 0.0)
            w_s = jnp.where(valid_s, jnp.exp(s_s - top), 0.0)
            total = jnp.sum(w, axis=-1, keepdims=True) + jnp.sum(
                w_s, axis=-1, keepdims=True
            )
            shifted = pltpu.roll(w, 1, 1).astype(jnp.bfloat16)
            odd = lax.broadcasted_iota(jnp.int32, (2 * SINKS, 2 * SINKS), 0) + 1
            move = jnp.where(
                odd == lax.broadcasted_iota(jnp.int32, (2 * SINKS, 2 * SINKS), 1),
                1.0, 0.0,
            ).astype(jnp.bfloat16)
            shifted_s = nn(w_s.astype(jnp.bfloat16), move).astype(jnp.bfloat16)
            weighted = nn(shifted, old) + nn(shifted_s, old_s)
            t = jnp.where(tree, nt(q, k) * scale, -1e30)
            joint = jnp.maximum(top, jnp.max(t, axis=-1, keepdims=True))
            tw = jnp.where(tree, jnp.exp(t - joint), 0.0)
            ratio = jnp.exp(top - joint)
            summed = nn(tw.astype(jnp.bfloat16), v)
            below = total * ratio + jnp.sum(tw, axis=-1, keepdims=True)
            att[:, cols] = ((weighted * ratio + summed) / below).astype(jnp.bfloat16)
            fresh_k[:, cols] = nn(pick[...], k).astype(jnp.bfloat16)
            fresh_v[:, cols] = nn(pick[...], v).astype(jnp.bfloat16)

        a = att[...]
        for t in range(TP):
            part[t] = nt(a, wo[t * WIDTH:(t + 1) * WIDTH, :]).astype(jnp.bfloat16)


def tail_kernel(part, fresh, P_out, G, own_sem, ps, pr, gs, gr):
    me = lax.axis_index("seq")
    lane = lax.axis_index("tp")
    barrier = pltpu.get_barrier_semaphore()

    def greet(k, carry):
        pl.semaphore_signal(barrier, 1, device_id={"seq": lax.rem(me + k, SEQ)})
        return carry

    lax.fori_loop(1, SEQ, greet, 0)
    for k in range(1, TP):
        pl.semaphore_signal(barrier, 1, device_id={"tp": lax.rem(lane + k, TP)})
    pl.semaphore_wait(barrier, SEQ + TP - 2)

    for k in range(1, TP):
        t = lax.rem(lane + k, TP)
        pltpu.make_async_remote_copy(
            src_ref=part.at[t], dst_ref=P_out.at[lane], send_sem=ps, recv_sem=pr,
            device_id={"tp": t},
        ).start()

    def scatter(k, carry):
        t = lax.rem(me + k, SEQ)
        pltpu.make_async_remote_copy(
            src_ref=fresh.at[t], dst_ref=G.at[me], send_sem=gs, recv_sem=gr,
            device_id={"seq": t},
        ).start()
        return carry

    lax.fori_loop(1, SEQ, scatter, 0)
    own_p = pltpu.make_async_copy(part.at[lane], P_out.at[lane], own_sem.at[0])
    own_g = pltpu.make_async_copy(fresh.at[me], G.at[me], own_sem.at[1])
    own_p.start()
    own_g.start()
    own_p.wait()
    own_g.wait()

    def all_of(ref, sem):
        pltpu.make_async_copy(ref, ref, sem).wait()

    all_of(P_out.at[pl.ds(0, TP - 1)], pr)
    all_of(G.at[pl.ds(0, SEQ - 1)], gr)
    all_of(part.at[pl.ds(0, TP - 1)], ps)
    all_of(fresh.at[pl.ds(0, SEQ - 1)], gs)


def final_kernel(deal, lengths, leaves, depth, P_in, G, cache, branch, new_cache):
    me = lax.axis_index("seq")
    total = P_in[0].astype(jnp.float32)
    for t in range(1, TP):
        total = total + P_in[t].astype(jnp.float32)
    branch[...] = total.astype(jnp.bfloat16)
    new_cache[...] = cache[...]

    def place(i, carry):
        r = deal[i]
        length = lengths[r]
        offset = lax.rem(me - length + 8 * SEQ, SEQ)

        @pl.when(offset <= depth[r, leaves[r]])
        def _():
            new_cache[r, lax.shift_right_logical(length + offset, 6)] = G[i]

        return carry

    lax.fori_loop(0, ROWS, place, 0)


def whole():
    return pl.BlockSpec(memory_space=pltpu.VMEM)


def shaped(shape, dtype=jnp.bfloat16):
    return jax.ShapeDtypeStruct(shape, dtype)


def run_pre(deal, lengths, leaves, tokens, parents, freq, cache):
    return pl.pallas_call(
        pre_kernel,
        name="pre",
        grid_spec=pltpu.PrefetchScalarGridSpec(
            num_scalar_prefetch=3,
            in_specs=[whole()] * 4,
            out_specs=[whole()] * 8,
            scratch_shapes=[pltpu.VMEM((ROWS, HD), jnp.int32)],
        ),
        out_shape=[
            shaped((SEQ, SLOTS, 2, WIDTH)),
            shaped((SEQ, 2, WIDTH)),
            shaped((ROWS, DEEP)),
            shaped((ROWS, ROWS), jnp.float32),
            shaped((ROWS, HD), jnp.float32),
            shaped((ROWS, HD), jnp.float32),
            shaped((SEQ, ROWS)),
            shaped((ROWS, HD), jnp.int32),
        ],
    )(deal, lengths, leaves, tokens, parents, freq, cache)


def run_comm(wq, wo, packed, sinks):
    dma = pltpu.SemaphoreType.DMA
    return pl.pallas_call(
        comm_kernel,
        name="comm",
        in_specs=[pl.BlockSpec(memory_space=pl.ANY)] * 4,
        out_specs=[pl.BlockSpec(memory_space=pl.ANY)] * 4,
        out_shape=[
            shaped((3, SEQ, DEEP // SEQ, WIDTH)),
            shaped((SEQ, DEEP // SEQ, WIDTH)),
            shaped((SEQ, SLOTS, 2, WIDTH)),
            shaped((SINKS, 2, WIDTH)),
        ],
        scratch_shapes=[
            dma((3,)), dma((X, Z)), dma((X, Z)),
            dma, dma, dma, dma, dma, dma, dma, dma, dma, dma,
        ],
        compiler_params=pltpu.CompilerParams(collective_id=0, has_side_effects=True),
    )(wq, wo, packed, sinks)


def run_main(deal, lengths, normed, wq, wo, kv, sk, reach, cos, sin, pick):
    steps = 8
    deep = DEEP // steps
    return pl.pallas_call(
        main_kernel,
        name="main",
        grid_spec=pltpu.PrefetchScalarGridSpec(
            num_scalar_prefetch=2,
            grid=(steps,),
            in_specs=[
                pl.BlockSpec((ROWS, deep), lambda i, *_: (0, i)),
                pl.BlockSpec((3, deep, WIDTH), lambda i, *_: (0, i, 0)),
                whole(), whole(), whole(), whole(), whole(), whole(), whole(),
            ],
            out_specs=[whole()] * 3,
            scratch_shapes=[
                pltpu.VMEM((3, ROWS, WIDTH), jnp.float32),
                pltpu.VMEM((ROWS, WIDTH), jnp.bfloat16),
            ],
        ),
        out_shape=[
            shaped((TP, ROWS, WIDTH)),
            shaped((SEQ, WIDTH)),
            shaped((SEQ, WIDTH)),
        ],
    )(deal, lengths, normed, wq, wo, kv, sk, reach, cos, sin, pick)


def run_tail(part, fresh):
    dma = pltpu.SemaphoreType.DMA
    return pl.pallas_call(
        tail_kernel,
        name="tail",
        in_specs=[pl.BlockSpec(memory_space=pl.ANY)] * 2,
        out_specs=[pl.BlockSpec(memory_space=pl.ANY)] * 2,
        out_shape=[shaped((TP, ROWS, WIDTH)), shaped((SEQ, 2, WIDTH))],
        scratch_shapes=[dma((2,)), dma, dma, dma, dma],
        compiler_params=pltpu.CompilerParams(collective_id=1, has_side_effects=True),
    )(part, fresh)


def run_final(deal, lengths, leaves, depth, gathered, arrived, cache):
    return pl.pallas_call(
        final_kernel,
        name="final",
        grid_spec=pltpu.PrefetchScalarGridSpec(
            num_scalar_prefetch=4,
            in_specs=[whole()] * 3,
            out_specs=[whole()] * 2,
        ),
        out_shape=[shaped((ROWS, WIDTH)), shaped(cache.shape)],
    )(deal, lengths, leaves, depth, gathered, arrived, cache)


def on_device(tokens, qkv_weight, out_weight, kv_cache, lengths, parents, leaves, deal):
    cache = kv_cache.reshape(kv_cache.shape[0], kv_cache.shape[1], 2, WIDTH)
    half = HD // 2
    freq = 10000.0 ** (-2.0 * jnp.arange(half, dtype=jnp.float32) / HD)
    freq = jnp.concatenate([freq, freq])[None, :]
    packed, sinks, normed, reach, cos, sin, pick, depth = run_pre(
        deal, lengths, leaves, tokens, parents, freq, cache
    )
    wq = jnp.transpose(qkv_weight, (1, 0, 2))
    wo = jnp.transpose(out_weight, (1, 0))
    all_q, all_o, kv, sk = run_comm(wq, wo, packed, sinks)
    part, fresh_k, fresh_v = run_main(
        deal, lengths, normed,
        all_q.reshape(3, DEEP, WIDTH), all_o.reshape(DEEP, WIDTH),
        kv.reshape(SEQ * SLOTS * 2, WIDTH), sk.reshape(2 * SINKS, WIDTH),
        reach, cos, sin, pick,
    )
    fresh = jnp.stack([fresh_k, fresh_v], axis=1)
    gathered, arrived = run_tail(part, fresh)
    branch, new_cache = run_final(deal, lengths, leaves, depth, gathered, arrived, cache)
    return branch, new_cache.reshape(kv_cache.shape)


def solution(mesh):
    placed = (
        P("seq", None),
        P("seq", None, "tp"),
        P("tp", "seq"),
        P(None, None, "seq", None, "tp"),
        P(),
        P(),
        P(),
        P(),
    )
    return jax.shard_map(
        on_device,
        mesh=mesh,
        in_specs=placed,
        out_specs=(P("seq", "tp"), P(None, None, "seq", None, "tp")),
        check_vma=False,
    )
```

time: 784 us -> 103 us (0.13)
  waiting for transfers between devices: 661 us -> 0 us
  Pallas kernels: 0 us -> 94.6 us
  local copies, waits for them, and re-layouts: 60.3 us -> 5.21 us
  matrix products: 20.7 us -> 0 us
  between operations: 19.1 us -> 0.66 us
  starting transfers between devices: 13.6 us -> 0 us
    all_gather x3 -> x0, waiting for transfers between devices: 231 us -> none  [the longest x1 82.3 us: on_device(): lax.all_gather(out_weight, 'seq', axis=1, tiled=True)]
    pmax x1 -> x0, waiting for transfers between devices: 174 us -> none  [on_device(): cache_peak = lax.pmax(jnp.max(masked, axis=-1), 'seq')]
    reduce_scatter x2 -> x0, waiting for transfers between devices: 154 us -> none  [the longest x1 154 us: on_device(): lax.psum_scatter(weighted_all.reshape(requests * rows, width_local), 'seq...]
    pallas_call x0 -> x5, Pallas kernels: none -> 94.6 us  [the longest x1 60.3 us: run_comm(): pl.pallas_call(comm_kernel, name='comm', in_specs=[pl.BlockSpec(memory_sp...]
    unnamed x8 -> x0, waiting for transfers between devices: 84.6 us -> none
    dot_general x13 -> x0, matrix products: 20.7 us -> none  [the longest x1 5.15 us: on_device(): jnp.einsum('rqhd,rchd->rqhc', slot_queries, blocks[:, :, 0], preferred_el...]
    all_to_all x2 -> x0, waiting for transfers between devices: 17.3 us -> none  [the longest x1 10.3 us: on_device(): lax.all_to_all(outgoing, 'seq', split_axis=0, concat_axis=0, tiled=True)]
    transpose x1 -> x0, local copies, waits for them, and re-layouts: 14.6 us -> none  [on_device(): jnp.einsum('rqhc,rchd->rqhd', weights.astype(jnp.bfloat16), blocks[:, :,...]
  transfers between devices with their start and end apart: 9 -> 0, of which waited for: 8 -> 0; matrix products, arithmetic and copies ran while one was open for 7% -> 0% of each run, Pallas kernels for 0% -> 0%
where the time goes in v1:
time: 103 us; the launch traced here: 102 us
  Pallas kernels  94.6 us (92%)
  local copies, waits for them, and re-layouts  5.21 us (5%)
  other arithmetic  1.56 us (2%)
    pallas_call x1, Pallas kernels, run_comm(): pl.pallas_call(comm_kernel, name='comm', in_specs=[pl.BlockSpec(memory_sp...  60.3 us
    pallas_call x1, Pallas kernels, run_tail(): pl.pallas_call(tail_kernel, name='tail', in_specs=[pl.BlockSpec(memory_sp...  12.9 us
    pallas_call x1, Pallas kernels, run_main(): pl.pallas_call(main_kernel, name='main', grid_spec=pltpu.PrefetchScalarGr...  11.5 us
    pallas_call x1, Pallas kernels, run_final(): pl.pallas_call(final_kernel, name='final', grid_spec=pltpu.PrefetchScalar...  5.19 us
    pallas_call x1, Pallas kernels, run_pre(): pl.pallas_call(pre_kernel, name='pre', grid_spec=pltpu.PrefetchScalarGrid...  4.69 us

profile of v1, /device:TPU:1, one launch (start us, length us, event | category | flops | bytes accessed | tf_op | source)
XLA Modules:
  0.0 102.0 jit_solution(3938003874540100413)
XLA Ops:
  0.6 0.6 maximum_bitcast_fusion.freq
  1.2 4.7 %pre.1 = (bf16[64,4,2,512]{3,2,1,0:T(2,128)(2,1)}, bf16[64,2,512]{2,1,0:T(2,128)(2,1)}, bf16[64,2048]{1,0:T(8,128)(2,1)}, f32[64,64]{1,0:T(8,128)}, f32[64,128]{...) custom-call(s32[64]{0:T(128)} %deal.5, s32[64]{0:T(128)} %lengths.5, s32[64]{0:T(128)} %leaves.3, ...), custom_call_target="tpu_custom_call" | custom-call | tf_op jit(solution)/shard_map/pre/pallas_call | solution.py:434
  5.9 60.3 %comm.1 = (bf16[3,64,32,512]{3,2,1,0:T(8,128)(2,1)}, bf16[64,32,512]{2,1,0:T(8,128)(2,1)}, bf16[64,4,2,512]{3,2,1,0:T(2,128)(2,1)}, bf16[4,2,512]{2,1,0:T(2,128)(2,1)}) custom-call(bf16[3,32,512]{2,1,0:T(8,128)(2,1)} %bitcast.16, bf16[32,512]{1,0:T(8,128)(2,1)} %bitcast.19, bf16[64,4,2,512]{3,2,1,0:T(2,128)(2,1)} %get-tuple-element.23.kv, ...), custom_call_target="tpu_custom_call" | custom-call | tf_op jit(solution)/shard_map/comm/pallas_call | solution.py:458
  66.2 1.3 %reshape.26.sk = bf16[8,512]{1,0:T(8,128)(2,1)} reshape(bf16[4,2,512]{2,1,0:T(2,128)(2,1)} %get-tuple-element.28) | data formatting | bytes 16384 | tf_op jit(solution)/shard_map/reshape | solution.py:545
  67.5 2.0 %reshape.25.kv = bf16[512,512]{1,0:T(8,128)(2,1)} reshape(bf16[64,4,2,512]{3,2,1,0:T(2,128)(2,1)} %get-tuple-element.27) | data formatting | bytes 1048576 | tf_op jit(solution)/shard_map/reshape | solution.py:545
  69.5 11.5 %main.1 = (bf16[4,64,512]{2,1,0:T(8,128)(2,1)}, bf16[64,512]{1,0:T(8,128)(2,1)}, bf16[64,512]{1,0:T(8,128)(2,1)}) custom-call(s32[64]{0:T(128)} %deal.5, s32[64]{0:T(128)} %lengths.5, bf16[64,2048]{1,0:T(8,128)(2,1)} %get-tuple-element.22.normed, bf16[3,2048,512]{2,1,0:T(8,128)(2,1)} %bitcast.12, bf16[2048,512]{1,0:T(8,128)(2,1)} %bitcast.15, ...), custom_call_target="tpu_custom_call" | custom-call | tf_op jit(solution)/shard_map/main/pallas_call | solution.py:480
  81.1 0.9 copy.11
  82.0 0.9 copy.12
  83.0 1.0 pad_maximum_fusion.fresh
  83.9 12.9 %tail.1 = (bf16[4,64,512]{2,1,0:T(8,128)(2,1)}, bf16[64,2,512]{2,1,0:T(2,128)(2,1)}) custom-call(bf16[4,64,512]{2,1,0:T(8,128)(2,1)} %get-tuple-element.33.part, bf16[64,2,512]{2,1,0:T(2,128)(2,1)} %pad_maximum_fusion.fresh), custom_call_target="tpu_custom_call" | custom-call | tf_op jit(solution)/shard_map/tail/pallas_call | solution.py:507
  96.8 5.2 %final.1 = (bf16[64,512]{1,0:T(8,128)(2,1)}, bf16[64,8,2,512]{3,2,1,0:T(2,128)(2,1)}) custom-call(s32[64]{0:T(128)} %deal.5, s32[64]{0:T(128)} %lengths.5, s32[64]{0:T(128)} %leaves.3, s32[64,128]{1,0:T(8,128)} %get-tuple-element.21.depth, bf16[4,64,512]{2,1,0:T(8,128)(2,1)} %get-tuple-element.36.P_in, bf16[64,2,512]{2,1,0:T(2,128)(2,1)} %get-tuple-element.37.G, ...), custom_call_target="tpu_custom_call" | custom-call | tf_op jit(solution)/shard_map/final/pallas_call | solution.py:519
  (1 shorter events, 0.0 us)

commit v2 on v1

v2 whole, which is shorter than its diff:
```python
import functools

import jax
import jax.numpy as jnp
from jax import lax
from jax.experimental import pallas as pl
from jax.experimental.pallas import tpu as pltpu
from jax.sharding import PartitionSpec as P

HD = 128
SINKS = 4
X, Z, CORES = 4, 8, 2
SEQ = X * Z * CORES
TP = 4
ROWS = 64
SLOTS = 4
WIDTH = 512
HEADS = WIDTH // HD
WINDOW = 256
DEEP = 2048
PROJ_AT = (10, 12, 14)


def nt(a, b):
    return lax.dot_general(
        a, b, (((1,), (1,)), ((), ())), preferred_element_type=jnp.float32
    )


def nn(a, b):
    return lax.dot_general(
        a, b, (((1,), (0,)), ((), ())), preferred_element_type=jnp.float32
    )


def whole_kernel(
    deal, lengths, leaves, tokens, parents, freq, cache, wq, wo,
    gathered, arrived, depth_out, cache_out,
    packed, sinks, WQ, WO, KV, SK, normed, acc, att, part, fresh, par_pad, G, PG,
    own_sem, ra, rb, sa, sb, sib_sa, sib_sb, sib_ra, sib_rb,
    kv_s, kv_r, sk_s, sk_r, ps, pr, gs, gr,
):
    me = lax.axis_index("seq")
    tp = lax.axis_index("tp")
    x = me // (Z * CORES)
    z = lax.rem(me // CORES, Z)
    c = lax.rem(me, CORES)

    def idx(dx, dz):
        return (
            lax.rem(x + (dx + X), X) * Z + lax.rem(z + (dz + Z), Z)
        ) * CORES + c

    barrier = pltpu.get_barrier_semaphore()

    def greet(k, carry):
        pl.semaphore_signal(barrier, 1, device_id={"seq": lax.rem(me + k, SEQ)})
        return carry

    lax.fori_loop(1, SEQ, greet, 0)
    for k in range(1, TP):
        pl.semaphore_signal(barrier, 1, device_id={"tp": lax.rem(tp + k, TP)})

    own_cache = pltpu.make_async_copy(cache, cache_out, own_sem.at[5])
    own_cache.start()
    own_a = pltpu.make_async_copy(wq, WQ.at[:, me], own_sem.at[0])
    own_b = pltpu.make_async_copy(wo, WO.at[me], own_sem.at[1])
    own_a.start()
    own_b.start()

    def pack(t, carry):
        r = deal[t]
        base = jnp.maximum(lengths[r] - WINDOW, 0)
        first = lax.shift_right_logical(base - me + (SEQ - 1), 6)
        packed[t] = cache[r, pl.ds(first, SLOTS)].reshape(2 * SLOTS, WIDTH)
        sinks[t] = cache[r, 0]
        return carry

    lax.fori_loop(0, ROWS, pack, 0)

    wide = tokens[...].astype(jnp.float32)
    centred = wide - jnp.mean(wide, axis=-1, keepdims=True)
    scaling = lax.rsqrt(jnp.mean(centred * centred, axis=-1, keepdims=True) + 1e-05)
    normed[...] = (centred * scaling).astype(jnp.bfloat16)
    acc[...] = jnp.zeros_like(acc)

    pl.semaphore_wait(barrier, SEQ + TP - 2)

    sibling = me + 1 - 2 * c
    to = {
        "x+": {"seq": idx(1, 0)},
        "x-": {"seq": idx(-1, 0)},
        "z+": {"seq": idx(0, 1)},
        "z-": {"seq": idx(0, -1)},
        "s": {"seq": sibling},
    }
    shift = {"x+": (-1, 0), "x-": (1, 0), "z+": (0, -1), "z-": (0, 1)}

    def send_a(dx, dz, way):
        at = idx(dx, dz)
        src = wq if (dx, dz) == (0, 0) else WQ.at[:, at]
        if way == "s":
            send, recv = sib_sa, sib_ra.at[dx % X]
        else:
            ox, oz = shift[way]
            send, recv = sa, ra.at[(dx + ox) % X, (dz + oz) % Z]
        pltpu.make_async_remote_copy(
            src_ref=src, dst_ref=WQ.at[:, at], send_sem=send, recv_sem=recv,
            device_id=to[way],
        ).start()

    def send_b(dx, dz, way):
        at = idx(dx, dz)
        src = wo if (dx, dz) == (0, 0) else WO.at[at]
        if way == "s":
            send, recv = sib_sb, sib_rb
        else:
            ox, oz = shift[way]
            send, recv = sb, rb.at[(dx + ox) % X, (dz + oz) % Z]
        pltpu.make_async_remote_copy(
            src_ref=src, dst_ref=WO.at[at], send_sem=send, recv_sem=recv,
            device_id=to[way],
        ).start()

    def wait_a(dx, dz):
        at = idx(dx, dz)
        pltpu.make_async_copy(
            WQ.at[:, at], WQ.at[:, at], ra.at[dx % X, dz % Z]
        ).wait()

    def wait_b(dx, dz):
        at = idx(dx, dz)
        pltpu.make_async_copy(WO.at[at], WO.at[at], rb.at[dx % X, dz % Z]).wait()

    def route_a(dx, dz):
        out = []
        if dx == 0:
            if dz == 0:
                out += ["z+", "z-"]
            elif -4 < dz < 0:
                out += ["z+"]
            elif 0 < dz < 3:
                out += ["z-"]
            out += ["x+", "x-"]
        elif dx == -1 and dz % 2 == 0:
            out += ["x+"]
        elif dx == 1 and dz % 2 == 1:
            out += ["x-"]
        return out + ["s"]

    def route_b(dx, dz):
        out = []
        if dz == 0:
            if dx == 0:
                out += ["x+", "x-"]
            elif dx == -1:
                out += ["x+"]
            out += ["z+", "z-"]
        else:
            far = 4 if dx % 2 == 0 else 3
            if -far < dz < 0:
                out += ["z+"]
            elif 0 < dz < 7 - far:
                out += ["z-"]
        return out + ["s"]

    def all_of(ref, sem):
        pltpu.make_async_copy(ref, ref, sem).wait()

    for way in route_a(0, 0):
        send_a(0, 0, way)
    for way in route_b(0, 0):
        send_b(0, 0, way)
    own_kv = pltpu.make_async_copy(packed.at[me], KV.at[me], own_sem.at[2])
    own_kv.start()

    def scatter(k, carry):
        t = lax.rem(me + k, SEQ)
        pltpu.make_async_remote_copy(
            src_ref=packed.at[t], dst_ref=KV.at[me], send_sem=kv_s, recv_sem=kv_r,
            device_id={"seq": t},
        ).start()
        return carry

    lax.fori_loop(1, SEQ, scatter, 0)

    @pl.when(me < SINKS)
    def _():
        pltpu.make_async_copy(sinks.at[me], SK.at[me], sk_r).start()

        def spread(k, carry):
            t = lax.rem(me + k, SEQ)
            pltpu.make_async_remote_copy(
                src_ref=sinks.at[t], dst_ref=SK.at[me], send_sem=sk_s, recv_sem=sk_r,
                device_id={"seq": t},
            ).start()
            return carry

        lax.fori_loop(1, SEQ, spread, 0)

    request = deal[me]
    length = lengths[request]
    leaf = leaves[request]
    sub = lax.broadcasted_iota(jnp.int32, (ROWS, ROWS), 0)
    lane = lax.broadcasted_iota(jnp.int32, (ROWS, ROWS), 1)
    eye = jnp.where(sub == lane, 1.0, 0.0)
    row = parents[pl.ds(request, 1), :]
    up = eye + jnp.where(row == sub, 1.0, 0.0)
    for _ in range(6):
        half = up.astype(jnp.bfloat16)
        up = jnp.minimum(nn(half, half), 1.0)
    reach = nt(eye.astype(jnp.bfloat16), up.astype(jnp.bfloat16))
    depth_row = (jnp.sum(up, axis=0, keepdims=True) - 1.0).astype(jnp.int32)
    depth_col = (jnp.sum(reach, axis=1, keepdims=True) - 1.0).astype(jnp.int32)
    places = (length + depth_col).astype(jnp.float32)
    angle = places * freq[...]
    cosine = jnp.cos(angle)
    wave = jnp.sin(angle)
    lanes = lax.broadcasted_iota(jnp.int32, (ROWS, HD), 1)
    sine = jnp.where(lanes < HD // 2, -wave, wave)
    on_path = jnp.sum(jnp.where(sub == leaf, reach, 0.0), axis=0, keepdims=True)
    offset = lax.rem(sub - length + 8 * SEQ, SEQ)
    hit = (on_path > 0.5) & (depth_row == offset)
    pick = jnp.where(hit, 1.0, 0.0).astype(jnp.bfloat16)

    par_pad[...] = lanes
    par_pad[:, 0:ROWS] = parents[...]
    par = par_pad[...]
    climb = jnp.where((lanes < ROWS) & (par >= 0), 1, 0)
    jump = jnp.where(par < 0, 0, par)
    for _ in range(6):
        climb = climb + jnp.take_along_axis(climb, jump, axis=1)
        jump = jnp.take_along_axis(jump, jump, axis=1)
    depth_out[...] = climb

    own_a.wait()
    own_b.wait()
    group = Z * CORES
    deep = group * (DEEP // SEQ)

    def project(dx, kind):
        block = lax.rem(x + (dx + X), X)
        left = normed[:, pl.ds(pl.multiple_of(block * deep, deep), deep)]
        right = WQ[kind, pl.ds(block * group, group)].reshape(deep, WIDTH)
        acc[kind] += nn(left, right)

    steps = []
    for dz in (-1, 1, -2, 2, -3, 3, -4):
        steps.append((2 * abs(dz), "a", 0, dz))
    for dx, cost in ((-1, 1), (1, 1), (-2, 2)):
        steps.append((2 * cost + 0.2, "b", dx, 0))
    for dz in (0, -1, 1, -2, 2, -3, 3, -4):
        for dx, cost in ((-1, 1), (1, 1), (-2, 2)):
            steps.append((2 * abs(dz) + 2 * cost + 0.5, "a", dx, dz))
    for dx in (0, -1, 1, -2):
        far = 4 if dx % 2 == 0 else 3
        for dz in list(range(-far, 0)) + list(range(1, 8 - far)):
            steps.append((2 * abs(dx) + 2 * abs(dz) + 0.6, "b", dx, dz))
    for turn, dx in enumerate((0, -1, 1)):
        for kind in range(3):
            steps.append((PROJ_AT[turn] + 0.7 + 0.01 * kind, "p", dx, kind))
    for _, kind, dx, dz in sorted(steps, key=lambda s: s[0]):
        if kind == "a":
            wait_a(dx, dz)
            for way in route_a(dx, dz):
                send_a(dx, dz, way)
        elif kind == "b":
            wait_b(dx, dz)
            for way in route_b(dx, dz):
                send_b(dx, dz, way)
        else:
            if dz == 0:
                all_of(WQ.at[:, pl.ds(0, Z)], sib_ra.at[dx % X])
            project(dx, dz)

    all_of(WQ.at[:, pl.ds(0, Z)], sib_ra.at[2])
    for kind in range(3):
        project(2, kind)

    def turn(v):
        return v * cosine + pltpu.roll(v, HD // 2, 1) * sine

    sides = [slice(h * HD, (h + 1) * HD) for h in range(HEADS)]
    keys, values = [], []
    twice = lax.broadcasted_iota(jnp.int32, (2 * SEQ, SEQ), 0)
    once = lax.broadcasted_iota(jnp.int32, (2 * SEQ, SEQ), 1)
    even = jnp.where(twice == 2 * once, 1.0, 0.0).astype(jnp.bfloat16)
    odd = jnp.where(twice == 2 * once + 1, 1.0, 0.0).astype(jnp.bfloat16)
    pick_k = nn(even, pick).astype(jnp.bfloat16)
    pick_v = nn(odd, pick).astype(jnp.bfloat16)
    for cols in sides:
        k = turn(acc[1, :, cols]).astype(jnp.bfloat16)
        v = acc[2, :, cols].astype(jnp.bfloat16)
        keys.append(k)
        values.append(v)
        mixed = (nn(pick_k, k) + nn(pick_v, v)).astype(jnp.bfloat16)
        fresh[:, :, cols] = mixed.reshape(SEQ, 2, HD)

    own_kv.wait()
    all_of(KV.at[pl.ds(0, SEQ - 1)], kv_r)
    all_of(SK, sk_r)

    scale = float(HD) ** (-0.5)
    base = jnp.maximum(length - WINDOW, 0)
    spot = lax.broadcasted_iota(jnp.int32, (ROWS, SEQ * SLOTS * 2), 1)
    shard = lax.shift_right_logical(spot, 3)
    slot = lax.shift_right_logical(spot & 7, 1)
    first = lax.shift_right_logical(base - shard + (SEQ - 1), 6)
    place = (first + slot) * SEQ + shard
    valid = (
        ((spot & 1) == 0)
        & (place < length)
        & ((place < SINKS) | (place >= length - WINDOW))
    )
    spot_s = lax.broadcasted_iota(jnp.int32, (ROWS, 2 * SINKS), 1)
    valid_s = ((spot_s & 1) == 0) & (
        length - WINDOW > lax.shift_right_logical(spot_s, 1)
    )
    tree = reach > 0.5
    small = (2 * SINKS, 2 * SINKS)
    move = jnp.where(
        lax.broadcasted_iota(jnp.int32, small, 0) + 1
        == lax.broadcasted_iota(jnp.int32, small, 1),
        1.0, 0.0,
    ).astype(jnp.bfloat16)

    def send_fresh():
        own_g = pltpu.make_async_copy(fresh.at[me], G.at[me], own_sem.at[4])
        own_g.start()

        def hand(k, carry):
            t = lax.rem(me + k, SEQ)
            pltpu.make_async_remote_copy(
                src_ref=fresh.at[t], dst_ref=G.at[me], send_sem=gs, recv_sem=gr,
                device_id={"seq": t},
            ).start()
            return carry

        lax.fori_loop(1, SEQ, hand, 0)
        return own_g

    for h, cols in enumerate(sides):
        q = turn(acc[0, :, cols]).astype(jnp.bfloat16)
        k, v = keys[h], values[h]
        old = KV[:, :, cols].reshape(SEQ * SLOTS * 2, HD)
        old_s = SK[:, :, cols].reshape(2 * SINKS, HD)
        s = jnp.where(valid, nt(q, old) * scale, -1e30)
        s_s = jnp.where(valid_s, nt(q, old_s) * scale, -1e30)
        top = jnp.maximum(
            jnp.max(s, axis=-1, keepdims=True), jnp.max(s_s, axis=-1, keepdims=True)
        )
        w = jnp.where(valid, jnp.exp(s - top), 0.0)
        w_s = jnp.where(valid_s, jnp.exp(s_s - top), 0.0)
        total = jnp.sum(w, axis=-1, keepdims=True) + jnp.sum(
            w_s, axis=-1, keepdims=True
        )
        shifted = pltpu.roll(w, 1, 1).astype(jnp.bfloat16)
        shifted_s = nn(w_s.astype(jnp.bfloat16), move).astype(jnp.bfloat16)
        weighted = nn(shifted, old) + nn(shifted_s, old_s)
        t = jnp.where(tree, nt(q, k) * scale, -1e30)
        joint = jnp.maximum(top, jnp.max(t, axis=-1, keepdims=True))
        tw = jnp.where(tree, jnp.exp(t - joint), 0.0)
        ratio = jnp.exp(top - joint)
        summed = nn(tw.astype(jnp.bfloat16), v)
        below = total * ratio + jnp.sum(tw, axis=-1, keepdims=True)
        att[:, cols] = ((weighted * ratio + summed) / below).astype(jnp.bfloat16)
        if h == 0:
            own_g = send_fresh()

    all_of(WO.at[pl.ds(0, SEQ // CORES)], sib_rb)
    a = att[...]
    wide_group = SEQ // TP
    for k in range(1, TP + 1):
        t = lax.rem(tp + k, TP)
        right = WO[pl.ds(t * wide_group, wide_group)].reshape(WIDTH, WIDTH)
        part[t] = nt(a, right).astype(jnp.bfloat16)
        if k > 1:
            t = lax.rem(tp + k - 1, TP)
            pltpu.make_async_remote_copy(
                src_ref=part.at[t], dst_ref=PG.at[tp], send_sem=ps, recv_sem=pr,
                device_id={"tp": t},
            ).start()
    own_p = pltpu.make_async_copy(part.at[tp], PG.at[tp], own_sem.at[3])
    own_p.start()

    others = pl.ds(0, SEQ - 1)
    pieces = SEQ // CORES
    all_of(WQ.at[:, pl.ds(0, pieces - 1)], sa)
    all_of(WO.at[pl.ds(0, pieces - 1)], sb)
    all_of(WQ.at[:, pl.ds(0, pieces)], sib_sa)
    all_of(WO.at[pl.ds(0, pieces)], sib_sb)
    all_of(packed.at[others], kv_s)

    @pl.when(me < SINKS)
    def _():
        all_of(sinks.at[others], sk_s)

    own_cache.wait()
    own_g.wait()
    all_of(G.at[others], gr)
    arrived[...] = G[...]
    own_p.wait()
    all_of(PG.at[pl.ds(0, TP - 1)], pr)
    below = PG[0].astype(jnp.float32)
    for t in range(1, TP):
        below = below + PG[t].astype(jnp.float32)
    gathered[...] = below.astype(jnp.bfloat16)
    all_of(part.at[pl.ds(0, TP - 1)], ps)
    all_of(fresh.at[others], gs)


def final_kernel(deal, lengths, leaves, depth, G, cache, new_cache, sems):
    me = lax.axis_index("seq")

    def each(act):
        def place(i, carry):
            r = deal[i]
            length = lengths[r]
            offset = lax.rem(me - length + 8 * SEQ, SEQ)

            @pl.when(offset <= depth[r, leaves[r]])
            def _():
                spot = lax.shift_right_logical(length + offset, 6)
                act(pltpu.make_async_copy(G.at[i], new_cache.at[r, spot], sems.at[i]))

            return carry

        lax.fori_loop(0, ROWS, place, 0)

    each(lambda copy: copy.start())
    each(lambda copy: copy.wait())


def whole():
    return pl.BlockSpec(memory_space=pltpu.VMEM)


def shaped(shape, dtype=jnp.bfloat16):
    return jax.ShapeDtypeStruct(shape, dtype)


def run_whole(deal, lengths, leaves, tokens, parents, freq, cache, wq, wo):
    dma = pltpu.SemaphoreType.DMA
    vmem = pltpu.VMEM
    half = jnp.bfloat16
    return pl.pallas_call(
        whole_kernel,
        name="whole",
        in_specs=[pl.BlockSpec(memory_space=pltpu.SMEM)] * 3 + [whole()] * 6,
        out_specs=[whole()] * 3 + [pl.BlockSpec(memory_space=pl.ANY)],
        out_shape=[
            shaped((ROWS, WIDTH)),
            shaped((SEQ, 2, WIDTH)),
            shaped((ROWS, HD), jnp.int32),
            shaped(cache.shape),
        ],
        scratch_shapes=[
            vmem((SEQ, 2 * SLOTS, WIDTH), half),
            vmem((SEQ, 2, WIDTH), half),
            vmem((3, SEQ, DEEP // SEQ, WIDTH), half),
            vmem((SEQ, DEEP // SEQ, WIDTH), half),
            vmem((SEQ, 2 * SLOTS, WIDTH), half),
            vmem((SINKS, 2, WIDTH), half),
            vmem((ROWS, DEEP), half),
            vmem((3, ROWS, WIDTH), jnp.float32),
            vmem((ROWS, WIDTH), half),
            vmem((TP, ROWS, WIDTH), half),
            vmem((SEQ, 2, WIDTH), half),
            vmem((ROWS, HD), jnp.int32),
            vmem((SEQ, 2, WIDTH), half),
            vmem((TP, ROWS, WIDTH), half),
            dma((6,)), dma((X, Z)), dma((X, Z)),
            dma, dma, dma, dma, dma((X,)), dma,
            dma, dma, dma, dma, dma, dma, dma, dma,
        ],
        compiler_params=pltpu.CompilerParams(collective_id=0, has_side_effects=True),
    )(deal, lengths, leaves, tokens, parents, freq, cache, wq, wo)


def run_final(deal, lengths, leaves, depth, arrived, cache):
    return pl.pallas_call(
        final_kernel,
        name="final",
        grid_spec=pltpu.PrefetchScalarGridSpec(
            num_scalar_prefetch=4,
            in_specs=[whole(), pl.BlockSpec(memory_space=pl.ANY)],
            out_specs=pl.BlockSpec(memory_space=pl.ANY),
            scratch_shapes=[pltpu.SemaphoreType.DMA((ROWS,))],
        ),
        out_shape=shaped(cache.shape),
        input_output_aliases={5: 0},
    )(deal, lengths, leaves, depth, arrived, cache)


def on_device(tokens, qkv_weight, out_weight, kv_cache, lengths, parents, leaves, deal):
    cache = kv_cache.reshape(kv_cache.shape[0], kv_cache.shape[1], 2, WIDTH)
    half = HD // 2
    freq = 10000.0 ** (-2.0 * jnp.arange(half, dtype=jnp.float32) / HD)
    freq = jnp.concatenate([freq, freq])[None, :]
    wq = jnp.transpose(qkv_weight, (1, 0, 2))
    wo = jnp.transpose(out_weight, (1, 0))
    branch, arrived, depth, copied = run_whole(
        deal, lengths, leaves, tokens, parents, freq, cache, wq, wo
    )
    new_cache = run_final(deal, lengths, leaves, depth, arrived, copied)
    return branch, new_cache.reshape(kv_cache.shape)


def solution(mesh):
    placed = (
        P("seq", None),
        P("seq", None, "tp"),
        P("tp", "seq"),
        P(None, None, "seq", None, "tp"),
        P(),
        P(),
        P(),
        P(),
    )
    return jax.shard_map(
        on_device,
        mesh=mesh,
        in_specs=placed,
        out_specs=(P("seq", "tp"), P(None, None, "seq", None, "tp")),
        check_vma=False,
    )
```

time: 103 us -> 81.4 us (0.79)
  Pallas kernels: 94.6 us -> 76.1 us
  local copies, waits for them, and re-layouts: 5.21 us -> 3.76 us
    pallas_call x4 -> x1, Pallas kernels: 89.4 us -> 71.9 us  [run_whole(): pl.pallas_call(whole_kernel, name='whole', in_specs=[pl.BlockSpec(memory_...]
    unnamed x0 -> x4, local copies, waits for them, and re-layouts: none -> 3.76 us
    reshape x2 -> x0, local copies, waits for them, and re-layouts: 3.33 us -> none  [the longest x1 2.03 us: on_device(): kv.reshape(SEQ * SLOTS * 2, WIDTH)]
    another operation x2 -> x0, local copies, waits for them, and re-layouts: 1.88 us -> none  [on_device(): fresh = jnp.stack([fresh_k, fresh_v], axis=1)]
where the time goes in v2:
time: 81.4 us; the launch traced here: 81.1 us
  Pallas kernels  76.1 us (93%)
  local copies, waits for them, and re-layouts  3.76 us (5%)
    pallas_call x1, Pallas kernels, run_whole(): pl.pallas_call(whole_kernel, name='whole', in_specs=[pl.BlockSpec(memory_...  71.9 us
    pallas_call x1, Pallas kernels, run_final(): pl.pallas_call(final_kernel, name='final', grid_spec=pltpu.PrefetchScalar...  4.16 us
    unnamed x4, local copies, waits for them, and re-layouts  3.76 us

profile of v2, /device:TPU:1, one launch (start us, length us, event | category | flops | bytes accessed | tf_op | source)
XLA Modules:
  0.0 81.1 jit_solution(12936580320279047882)
XLA Ops:
  0.6 0.6 maximum_bitcast_fusion.freq
  1.2 71.9 %whole.1 = (bf16[64,512]{1,0:T(8,128)(2,1)}, bf16[64,2,512]{2,1,0:T(2,128)(2,1)}, s32[64,128]{1,0:T(8,128)}, bf16[64,8,2,512]{3,2,1,0:T(2,128)(2,1)}) custom-call(s32[64]{0:T(128)} %deal.3, s32[64]{0:T(128)} %lengths.3, s32[64]{0:T(128)} %leaves.3, bf16[64,2048]{1,0:T(8,128)(2,1)} %tokens.1, s32[64,64]{1,0:T(8,128)} %parents.1, ...), custom_call_target="tpu_custom_call" | custom-call | tf_op jit(solution)/shard_map/whole/pallas_call | solution.py:446
  73.1 0.0 copy-start
  73.2 4.2 %final.1 = bf16[64,8,2,512]{3,2,1,0:T(2,128)(2,1)} custom-call(s32[64]{0:T(128)} %deal.3, s32[64]{0:T(128)} %lengths.3, s32[64]{0:T(128)} %leaves.3, s32[64,128]{1,0:T(8,128)} %get-tuple-element.7.depth, bf16[64,2,512]{2,1,0:T(2,128)(2,1)} %get-tuple-element.8.G, bf16[64,8,2,512]{3,2,1,0:T(2,128)(2,1)} %get-tuple-element.9.cache), custom_call_target="tpu_custom_call", output_to_operand_aliasing={{}: (5, {})} | custom-call | tf_op jit(solution)/shard_map/final/pallas_call | solution.py:481
  77.3 0.0 copy-done
  77.3 0.6 copy.15
  78.0 3.1 %copy.16 = bf16[64,8,1,2,512]{4,3,2,1,0:T(2,128)(2,1)} copy(bf16[64,8,1,2,512]{4,3,2,1,0:T(2,128)(2,1)} %bitcast.8) | data formatting | bytes 2097152
  (1 shorter events, 0.0 us)
Async XLA Ops:
  73.1 4.2 %copy-start = (bf16[64,512]{1,0:T(8,128)(2,1)S(1)}, bf16[64,512]{1,0:T(8,128)(2,1)}, u32[]{:S(2)}) copy-start(bf16[64,512]{1,0:T(8,128)(2,1)} %get-tuple-element.14) | copy-start | bytes 196612

commit v3 on v2

--- a/solution.py
+++ b/solution.py
@@ -2,6 +2,7 @@
 
 import jax
 import jax.numpy as jnp
+import numpy as np
 from jax import lax
 from jax.experimental import pallas as pl
 from jax.experimental.pallas import tpu as pltpu
@@ -19,6 +20,8 @@
 WINDOW = 256
 DEEP = 2048
 PROJ_AT = (10, 12, 14)
+KV_PARTS = tuple((low, min(low + 8, SEQ)) for low in range(1, SEQ, 8))
+KV_AT = (7.1, 8.1, 8.8, 9.4, 10.1, 10.8, 11.1, 11.6)
 
 
 def nt(a, b):
@@ -34,8 +37,8 @@
 
 
 def whole_kernel(
-    deal, lengths, leaves, tokens, parents, freq, cache, wq, wo,
-    gathered, arrived, depth_out, cache_out,
+    deal, lengths, leaves, tokens, parents, freq, spans, tips, cache, wq, wo,
+    gathered, arrived, code_out,
     packed, sinks, WQ, WO, KV, SK, normed, acc, att, part, fresh, par_pad, G, PG,
     own_sem, ra, rb, sa, sb, sib_sa, sib_sb, sib_ra, sib_rb,
     kv_s, kv_r, sk_s, sk_r, ps, pr, gs, gr,
@@ -61,8 +64,6 @@
     for k in range(1, TP):
         pl.semaphore_signal(barrier, 1, device_id={"tp": lax.rem(tp + k, TP)})
 
-    own_cache = pltpu.make_async_copy(cache, cache_out, own_sem.at[5])
-    own_cache.start()
     own_a = pltpu.make_async_copy(wq, WQ.at[:, me], own_sem.at[0])
     own_b = pltpu.make_async_copy(wo, WO.at[me], own_sem.at[1])
     own_a.start()
@@ -181,8 +182,6 @@
             device_id={"seq": t},
         ).start()
         return carry
-
-    lax.fori_loop(1, SEQ, scatter, 0)
 
     @pl.when(me < SINKS)
     def _():
@@ -231,7 +230,14 @@
     for _ in range(6):
         climb = climb + jnp.take_along_axis(climb, jump, axis=1)
         jump = jnp.take_along_axis(jump, jump, axis=1)
-    depth_out[...] = climb
+    tip = jnp.sum(jnp.where(sub == lane, tips[...], 0), axis=1, keepdims=True)
+    span = jnp.sum(jnp.where(sub == lane, spans[...], 0), axis=1, keepdims=True)
+    end = jnp.sum(jnp.where(lanes == tip, climb, 0), axis=1, keepdims=True)
+    ahead = (me - span + 8 * SEQ) & (SEQ - 1)
+    code = jnp.where(
+        ahead <= end, lax.shift_right_logical(span + ahead, 6), -1
+    )
+    code_out[...] = jnp.sum(jnp.where(sub == lane, code, 0), axis=0, keepdims=True)
 
     own_a.wait()
     own_b.wait()
@@ -256,6 +262,8 @@
         far = 4 if dx % 2 == 0 else 3
         for dz in list(range(-far, 0)) + list(range(1, 8 - far)):
             steps.append((2 * abs(dx) + 2 * abs(dz) + 0.6, "b", dx, dz))
+    for turn, (low, high) in enumerate(KV_PARTS):
+        steps.append((KV_AT[turn], "k", low, high))
     for turn, dx in enumerate((0, -1, 1)):
         for kind in range(3):
             steps.append((PROJ_AT[turn] + 0.7 + 0.01 * kind, "p", dx, kind))
@@ -268,6 +276,8 @@
             wait_b(dx, dz)
             for way in route_b(dx, dz):
                 send_b(dx, dz, way)
+        elif kind == "k":
+            lax.fori_loop(dx, dz, scatter, 0)
         else:
             if dz == 0:
                 all_of(WQ.at[:, pl.ds(0, Z)], sib_ra.at[dx % X])
@@ -395,7 +405,6 @@
     def _():
         all_of(sinks.at[others], sk_s)
 
-    own_cache.wait()
     own_g.wait()
     all_of(G.at[others], gr)
     arrived[...] = G[...]
@@ -409,26 +418,22 @@
     all_of(fresh.at[others], gs)
 
 
-def final_kernel(deal, lengths, leaves, depth, G, cache, new_cache, sems):
-    me = lax.axis_index("seq")
-
-    def each(act):
-        def place(i, carry):
-            r = deal[i]
-            length = lengths[r]
-            offset = lax.rem(me - length + 8 * SEQ, SEQ)
-
-            @pl.when(offset <= depth[r, leaves[r]])
-            def _():
-                spot = lax.shift_right_logical(length + offset, 6)
-                act(pltpu.make_async_copy(G.at[i], new_cache.at[r, spot], sems.at[i]))
-
-            return carry
-
-        lax.fori_loop(0, ROWS, place, 0)
-
-    each(lambda copy: copy.start())
-    each(lambda copy: copy.wait())
+def final_kernel(deal, code, G, cache, new_cache, sem):
+    copy = pltpu.make_async_copy(cache, new_cache, sem)
+    copy.start()
+    copy.wait()
+
+    def place(i, carry):
+        r = deal[i]
+        spot = code[0, r]
+
+        @pl.when(spot >= 0)
+        def _():
+            new_cache[r, spot] = G[i]
+
+        return carry
+
+    lax.fori_loop(0, ROWS, place, 0, unroll=8)
 
 
 def whole():
@@ -439,20 +444,19 @@
     return jax.ShapeDtypeStruct(shape, dtype)
 
 
-def run_whole(deal, lengths, leaves, tokens, parents, freq, cache, wq, wo):
+def run_whole(deal, lengths, leaves, tokens, parents, freq, spans, tips, cache, wq, wo):
     dma = pltpu.SemaphoreType.DMA
     vmem = pltpu.VMEM
     half = jnp.bfloat16
     return pl.pallas_call(
         whole_kernel,
         name="whole",
-        in_specs=[pl.BlockSpec(memory_space=pltpu.SMEM)] * 3 + [whole()] * 6,
-        out_specs=[whole()] * 3 + [pl.BlockSpec(memory_space=pl.ANY)],
+        in_specs=[pl.BlockSpec(memory_space=pltpu.SMEM)] * 3 + [whole()] * 8,
+        out_specs=[whole()] * 3,
         out_shape=[
             shaped((ROWS, WIDTH)),
             shaped((SEQ, 2, WIDTH)),
-            shaped((ROWS, HD), jnp.int32),
-            shaped(cache.shape),
+            shaped((1, ROWS), jnp.int32),
         ],
         scratch_shapes=[
             vmem((SEQ, 2 * SLOTS, WIDTH), half),
@@ -474,35 +478,34 @@
             dma, dma, dma, dma, dma, dma, dma, dma,
         ],
         compiler_params=pltpu.CompilerParams(collective_id=0, has_side_effects=True),
-    )(deal, lengths, leaves, tokens, parents, freq, cache, wq, wo)
-
-
-def run_final(deal, lengths, leaves, depth, arrived, cache):
+    )(deal, lengths, leaves, tokens, parents, freq, spans, tips, cache, wq, wo)
+
+
+def run_final(deal, code, arrived, cache):
     return pl.pallas_call(
         final_kernel,
         name="final",
         grid_spec=pltpu.PrefetchScalarGridSpec(
-            num_scalar_prefetch=4,
+            num_scalar_prefetch=2,
             in_specs=[whole(), pl.BlockSpec(memory_space=pl.ANY)],
-            out_specs=pl.BlockSpec(memory_space=pl.ANY),
-            scratch_shapes=[pltpu.SemaphoreType.DMA((ROWS,))],
+            out_specs=whole(),
+            scratch_shapes=[pltpu.SemaphoreType.DMA],
         ),
         out_shape=shaped(cache.shape),
-        input_output_aliases={5: 0},
-    )(deal, lengths, leaves, depth, arrived, cache)
+    )(deal, code, arrived, cache)
 
 
 def on_device(tokens, qkv_weight, out_weight, kv_cache, lengths, parents, leaves, deal):
     cache = kv_cache.reshape(kv_cache.shape[0], kv_cache.shape[1], 2, WIDTH)
-    half = HD // 2
-    freq = 10000.0 ** (-2.0 * jnp.arange(half, dtype=jnp.float32) / HD)
-    freq = jnp.concatenate([freq, freq])[None, :]
+    half = np.arange(HD, dtype=np.float64) % (HD // 2)
+    freq = jnp.asarray((10000.0 ** (-2.0 * half / HD)).astype(np.float32)[None, :])
     wq = jnp.transpose(qkv_weight, (1, 0, 2))
     wo = jnp.transpose(out_weight, (1, 0))
-    branch, arrived, depth, copied = run_whole(
-        deal, lengths, leaves, tokens, parents, freq, cache, wq, wo
-    )
-    new_cache = run_final(deal, lengths, leaves, depth, arrived, copied)
+    branch, arrived, code = run_whole(
+        deal, lengths, leaves, tokens, parents, freq,
+        lengths.reshape(1, ROWS), leaves.reshape(1, ROWS), cache, wq, wo,
+    )
+    new_cache = run_final(deal, code, arrived, cache)
     return branch, new_cache.reshape(kv_cache.shape)
 
 

time: 81.4 us -> 72.8 us (0.89)
  Pallas kernels: 76.1 us -> 71.2 us
  local copies, waits for them, and re-layouts: 3.76 us -> 0.64 us
    pallas_call x1, Pallas kernels: 71.9 us -> 66.9 us  [run_whole(): pl.pallas_call(whole_kernel, name='whole', in_specs=[pl.BlockSpec(memory_...]
    unnamed x4 -> x3, local copies, waits for them, and re-layouts: 3.76 us -> 0.64 us
where the time goes in v3:
time: 72.8 us; the launch traced here: 72.5 us
  Pallas kernels  71.2 us (98%)
    pallas_call x1, Pallas kernels, run_whole(): pl.pallas_call(whole_kernel, name='whole', in_specs=[pl.BlockSpec(memory_...  66.9 us
    pallas_call x1, Pallas kernels, run_final(): pl.pallas_call(final_kernel, name='final', grid_spec=pltpu.PrefetchScalar...  4.27 us

profile of v3, /device:TPU:1, one launch (start us, length us, event | category | flops | bytes accessed | tf_op | source)
XLA Modules:
  0.0 72.5 jit_solution(5653753996960452803)
XLA Ops:
  0.6 66.9 %whole.1 = (bf16[64,512]{1,0:T(8,128)(2,1)}, bf16[64,2,512]{2,1,0:T(2,128)(2,1)}, s32[1,64]{1,0:T(1,128)}) custom-call(s32[64]{0:T(128)} %deal.3, s32[64]{0:T(128)} %lengths.1, s32[64]{0:T(128)} %leaves.1, bf16[64,2048]{1,0:T(8,128)(2,1)} %tokens.1, s32[64,64]{1,0:T(8,128)} %parents.1, f32[1,128]{1,0:T(1,128)} %constant.2.clone.freq, s32[1,64]{1,0:T(1,128)} %bitcast.13, ...), custom_call_target="tpu_custom_call" | custom-call | tf_op jit(solution)/shard_map/whole/pallas_call | solution.py:451
  67.6 0.0 copy-start
  67.6 4.3 %final.1 = bf16[64,8,2,512]{3,2,1,0:T(2,128)(2,1)} custom-call(s32[64]{0:T(128)} %deal.3, s32[1,64]{1,0:T(1,128)} %get-tuple-element.6.code, bf16[64,2,512]{2,1,0:T(2,128)(2,1)} %get-tuple-element.7.G, bf16[64,8,2,512]{3,2,1,0:T(2,128)(2,1)} %bitcast.9), custom_call_target="tpu_custom_call" | custom-call | tf_op jit(solution)/shard_map/final/pallas_call | solution.py:485
  71.9 0.0 copy-done
  71.9 0.6 copy.13
Async XLA Ops:
  67.6 4.3 %copy-start = (bf16[64,512]{1,0:T(8,128)(2,1)S(1)}, bf16[64,512]{1,0:T(8,128)(2,1)}, u32[]{:S(2)}) copy-start(bf16[64,512]{1,0:T(8,128)(2,1)} %get-tuple-element.12) | copy-start | bytes 196612

commit v4 on v3

v4 whole, which is shorter than its diff:
```python
import functools

import jax
import jax.numpy as jnp
import numpy as np
from jax import lax
from jax.experimental import pallas as pl
from jax.experimental.pallas import tpu as pltpu
from jax.sharding import PartitionSpec as P

HD = 128
SINKS = 4
X, Z, CORES = 4, 8, 2
SEQ = X * Z * CORES
TP = 4
COLUMN = Z * CORES
ROWS = 64
SLOTS = 4
WIDTH = 512
HEADS = WIDTH // HD
WINDOW = 256
DEEP = 2048
KV_PARTS = ((1, 16), (16, 28), (28, 40), (40, 52), (52, 64))


def nt(a, b):
    return lax.dot_general(
        a, b, (((1,), (1,)), ((), ())), preferred_element_type=jnp.float32
    )


def nn(a, b):
    return lax.dot_general(
        a, b, (((1,), (0,)), ((), ())), preferred_element_type=jnp.float32
    )


def whole_kernel(
    deal, lengths, leaves, tokens, parents, freq, spans, tips, cache, wq, wo,
    gathered, arrived, code_out,
    packed, sinks, N, WH, WO, KV, SK, acc, att, ATT, part, PG, fresh, G, par_pad,
    own_sem, tr, wr, br,
    t_s, wx_s, wx_r, w_s, wsib_s, wsib_r, b_s, bsib_s, bsib_r,
    kv_s, kv_r, sk_s, sk_r, a_s, a_r, ps, pr, gs, gr,
):
    me = lax.axis_index("seq")
    tp = lax.axis_index("tp")
    x = me // COLUMN
    z = lax.rem(me // CORES, Z)
    c = lax.rem(me, CORES)
    column = lax.rem(me, COLUMN)

    def xat(dx):
        return lax.rem(x + (dx + X), X)

    def qat(dz):
        return lax.rem(z + (dz + Z), Z) * CORES + c

    def idx(dx, dz):
        return xat(dx) * COLUMN + qat(dz)

    def side(h):
        return pl.ds(pl.multiple_of(h * HD, HD), HD)

    def all_of(ref, sem):
        pltpu.make_async_copy(ref, ref, sem).wait()

    def send(src, dst, there, here, target):
        pltpu.make_async_remote_copy(
            src_ref=src, dst_ref=dst, send_sem=there, recv_sem=here,
            device_id={"seq": target},
        ).start()

    barrier = pltpu.get_barrier_semaphore()

    def greet(k, carry):
        pl.semaphore_signal(barrier, 1, device_id={"seq": lax.rem(me + k, SEQ)})
        return carry

    lax.fori_loop(1, SEQ, greet, 0)
    for k in range(1, TP):
        pl.semaphore_signal(barrier, 1, device_id={"tp": lax.rem(tp + k, TP)})

    own_w = pltpu.make_async_copy(
        wq.at[:, :, side(x)], WH.at[:, x, column], own_sem.at[0]
    )
    own_w.start()
    own_b = pltpu.make_async_copy(wo, WO.at[me], own_sem.at[1])
    own_b.start()

    wide = tokens[...].astype(jnp.float32)
    centred = wide - jnp.mean(wide, axis=-1, keepdims=True)
    scaling = lax.rsqrt(jnp.mean(centred * centred, axis=-1, keepdims=True) + 1e-05)
    N[x] = (centred * scaling).astype(jnp.bfloat16)

    def pack(t, carry):
        r = deal[t]
        base = jnp.maximum(lengths[r] - WINDOW, 0)
        first = lax.shift_right_logical(base - me + (SEQ - 1), 6)
        rows = cache[r, pl.ds(first, SLOTS)].reshape(2 * SLOTS, WIDTH)
        sunk = cache[r, 0]
        far, near = t // COLUMN, lax.rem(t, COLUMN)
        for h in range(HEADS):
            packed[h * COLUMN + near, far] = rows[:, h * HD:(h + 1) * HD]
            sinks[h * COLUMN + near, far] = sunk[:, h * HD:(h + 1) * HD]
        return carry

    lax.fori_loop(0, ROWS, pack, 0)

    pl.semaphore_wait(barrier, SEQ + TP - 2)

    for k in (2, 1, 3):
        send(
            wq.at[:, :, side(xat(k))], WH.at[:, x, column], wx_s, wx_r, idx(k, 0)
        )
    send(N.at[x], N.at[x], t_s, tr.at[0], idx(1, 0))
    send(N.at[x], N.at[x], t_s, tr.at[1], idx(-1, 0))

    own_kv = pltpu.make_async_copy(packed.at[me], KV.at[me], own_sem.at[2])
    own_kv.start()

    def scatter(low, high):
        def one(k, carry):
            t = lax.rem(me + k, SEQ)
            send(packed.at[t], KV.at[me], kv_s, kv_r, t)
            return carry

        lax.fori_loop(low, high, one, 0)

    scatter(*KV_PARTS[0])

    sub = lax.broadcasted_iota(jnp.int32, (ROWS, ROWS), 0)
    lane = lax.broadcasted_iota(jnp.int32, (ROWS, ROWS), 1)
    lanes = lax.broadcasted_iota(jnp.int32, (ROWS, HD), 1)
    eye = jnp.where(sub == lane, 1.0, 0.0)

    def describe(k):
        request = deal[xat(k) * COLUMN + column]
        length = lengths[request]
        leaf = leaves[request]
        row = parents[pl.ds(request, 1), :]
        up = eye + jnp.where(row == sub, 1.0, 0.0)
        for _ in range(6):
            half = up.astype(jnp.bfloat16)
            up = jnp.minimum(nn(half, half), 1.0)
        reach = nt(eye.astype(jnp.bfloat16), up.astype(jnp.bfloat16))
        depth_row = (jnp.sum(up, axis=0, keepdims=True) - 1.0).astype(jnp.int32)
        depth_col = (jnp.sum(reach, axis=1, keepdims=True) - 1.0).astype(jnp.int32)
        angle = (length + depth_col).astype(jnp.float32) * freq[...]
        cosine = jnp.cos(angle)
        wave = jnp.sin(angle)
        sine = jnp.where(lanes < HD // 2, -wave, wave)
        on_path = jnp.sum(jnp.where(sub == leaf, reach, 0.0), axis=0, keepdims=True)
        offset = lax.rem(sub - length + 8 * SEQ, SEQ)
        hit = (on_path > 0.5) & (depth_row == offset)
        pick = jnp.where(hit, 1.0, 0.0).astype(jnp.bfloat16)
        return length, reach, cosine, sine, pick

    def table():
        par_pad[...] = lanes
        par_pad[:, 0:ROWS] = parents[...]
        par = par_pad[...]
        climb = jnp.where((lanes < ROWS) & (par >= 0), 1, 0)
        jump = jnp.where(par < 0, 0, par)
        for _ in range(6):
            climb = climb + jnp.take_along_axis(climb, jump, axis=1)
            jump = jnp.take_along_axis(jump, jump, axis=1)
        tip = jnp.sum(jnp.where(sub == lane, tips[...], 0), axis=1, keepdims=True)
        span = jnp.sum(jnp.where(sub == lane, spans[...], 0), axis=1, keepdims=True)
        end = jnp.sum(jnp.where(lanes == tip, climb, 0), axis=1, keepdims=True)
        ahead = (me - span + 8 * SEQ) & (SEQ - 1)
        code = jnp.where(
            ahead <= end, lax.shift_right_logical(span + ahead, 6), -1
        )
        code_out[...] = jnp.sum(
            jnp.where(sub == lane, code, 0), axis=0, keepdims=True
        )

    def send_w(dz, step):
        at = WH.at[:, :, qat(dz)]
        if step == 0:
            send(at, at, wsib_s, wsib_r, me + 1 - 2 * c)
        else:
            send(at, at, w_s, wr.at[(dz - step) % Z], idx(0, step))

    def hop_w(dz):
        at = WH.at[:, :, qat(dz)]
        all_of(at, wr.at[dz % Z])
        if -4 < dz < 0:
            send_w(dz, 1)
        elif 0 < dz < 3:
            send_w(dz, -1)
        send_w(dz, 0)

    def send_b(dx, dz, way):
        at = idx(dx, dz)
        src = wo if (dx, dz) == (0, 0) else WO.at[at]
        if way == "s":
            send(src, WO.at[at], bsib_s, bsib_r, me + 1 - 2 * c)
        else:
            ox, oz = {"x+": (1, 0), "x-": (-1, 0), "z+": (0, 1), "z-": (0, -1)}[way]
            send(
                src, WO.at[at], b_s, br.at[(dx - ox) % X, (dz - oz) % Z], idx(ox, oz)
            )

    def hop_b(dx, dz):
        if (dx, dz) != (0, 0):
            all_of(WO.at[idx(dx, dz)], br.at[dx % X, dz % Z])
        out = []
        if dx == 0:
            if dz == 0:
                out += ["z+", "z-"]
            elif -4 < dz < 0:
                out += ["z+"]
            elif 0 < dz < 3:
                out += ["z-"]
            out += ["x+", "x-"]
        elif dx == -1 and dz % 2 == 0:
            out += ["x+"]
        elif dx == 1 and dz % 2 == 1:
            out += ["x-"]
        for way in out + ["s"]:
            send_b(dx, dz, way)

    order = (2, 1, 3, 0)
    told = {order[0]: describe(order[0])}

    own_w.wait()
    all_of(WH.at[:, pl.ds(0, X - 1), 0], wx_r)
    send_w(0, 1)
    send_w(0, -1)
    send_w(0, 0)
    scatter(*KV_PARTS[1])
    told[order[1]] = describe(order[1])

    left, right = pl.ds(0, DEEP // 2), pl.ds(DEEP // 2, DEEP // 2)
    all_of(N.at[0], tr.at[0])
    at = N.at[xat(-1), :, left]
    send(at, at, t_s, tr.at[2], idx(1, 0))
    all_of(N.at[0], tr.at[1])
    at = N.at[xat(1), :, right]
    send(at, at, t_s, tr.at[3], idx(-1, 0))

    hop_w(-1)
    hop_w(1)
    scatter(*KV_PARTS[2])

    @pl.when(me < SINKS)
    def _():
        pltpu.make_async_copy(sinks.at[me], SK.at[me], sk_r).start()

        def spread(k, carry):
            t = lax.rem(me + k, SEQ)
            send(sinks.at[t], SK.at[me], sk_s, sk_r, t)
            return carry

        lax.fori_loop(1, SEQ, spread, 0)

    told[order[2]] = describe(order[2])
    hop_w(-2)
    hop_w(2)
    scatter(*KV_PARTS[3])
    told[order[3]] = describe(order[3])
    hop_w(-3)
    hop_w(3)
    scatter(*KV_PARTS[4])
    own_b.wait()
    hop_b(0, 0)
    table()
    hop_w(-4)

    all_of(N.at[0, :, left], tr.at[2])
    all_of(N.at[0, :, right], tr.at[3])
    hop_b(0, -1)
    hop_b(0, 1)
    all_of(WH.at[:, :, pl.ds(0, Z)], wsib_r)
    deep = COLUMN * (DEEP // SEQ)
    rows_all = X * ROWS
    for kind in range(3):
        total = None
        for block in range(X):
            mine = N[:, :, block * deep:(block + 1) * deep].reshape(rows_all, deep)
            term = nn(mine, WH[kind, block].reshape(deep, HD))
            total = term if total is None else total + term
        acc[kind] = total
        if kind == 0:
            hop_b(0, -2)
            hop_b(0, 2)

    twice = lax.broadcasted_iota(jnp.int32, (2 * SEQ, SEQ), 0)
    once = lax.broadcasted_iota(jnp.int32, (2 * SEQ, SEQ), 1)
    even = jnp.where(twice == 2 * once, 1.0, 0.0).astype(jnp.bfloat16)
    odd = jnp.where(twice == 2 * once + 1, 1.0, 0.0).astype(jnp.bfloat16)

    def block_rows(kind, k):
        return acc[kind, pl.ds(pl.multiple_of(xat(k) * ROWS, ROWS), ROWS)]

    keys, values = {}, {}
    for k in order:
        _, _, cosine, sine, pick = told[k]
        key = block_rows(1, k)
        key = key * cosine + pltpu.roll(key, HD // 2, 1) * sine
        keys[k] = key.astype(jnp.bfloat16)
        values[k] = block_rows(2, k).astype(jnp.bfloat16)
        pick_k = nn(even, pick).astype(jnp.bfloat16)
        pick_v = nn(odd, pick).astype(jnp.bfloat16)
        mixed = (nn(pick_k, keys[k]) + nn(pick_v, values[k])).astype(jnp.bfloat16)
        fresh[:, xat(k)] = mixed.reshape(SEQ, 2, HD)
    hop_b(0, -3)
    hop_b(0, 3)

    own_g = pltpu.make_async_copy(fresh.at[me], G.at[me], own_sem.at[4])
    own_g.start()

    def hand(k, carry):
        t = lax.rem(me + k, SEQ)
        send(fresh.at[t], G.at[me], gs, gr, t)
        return carry

    lax.fori_loop(1, SEQ, hand, 0)

    later = [(dx, dz) for dz in (0, -1, 1, -2, 2, -3, 3, -4) for dx in (-1, 1)]
    later.insert(8, (0, -4))
    parts = [later[0:4], later[4:9], later[9:13], later[13:17]]

    own_kv.wait()
    all_of(KV.at[pl.ds(0, SEQ - 1)], kv_r)
    all_of(SK, sk_r)

    scale = float(HD) ** (-0.5)
    spot = lax.broadcasted_iota(jnp.int32, (ROWS, SEQ * SLOTS * 2), 1)
    shard = lax.shift_right_logical(spot, 3)
    slot = lax.shift_right_logical(spot & 7, 1)
    spot_s = lax.broadcasted_iota(jnp.int32, (ROWS, 2 * SINKS), 1)
    small = (2 * SINKS, 2 * SINKS)
    move = jnp.where(
        lax.broadcasted_iota(jnp.int32, small, 0) + 1
        == lax.broadcasted_iota(jnp.int32, small, 1),
        1.0, 0.0,
    ).astype(jnp.bfloat16)

    for turn, k in enumerate(order):
        length, reach, cosine, sine, _ = told[k]
        base = jnp.maximum(length - WINDOW, 0)
        first = lax.shift_right_logical(base - shard + (SEQ - 1), 6)
        place = (first + slot) * SEQ + shard
        valid = (
            ((spot & 1) == 0)
            & (place < length)
            & ((place < SINKS) | (place >= length - WINDOW))
        )
        valid_s = ((spot_s & 1) == 0) & (
            length - WINDOW > lax.shift_right_logical(spot_s, 1)
        )
        q = block_rows(0, k)
        q = (q * cosine + pltpu.roll(q, HD // 2, 1) * sine).astype(jnp.bfloat16)
        old = KV[:, pl.ds(xat(k), 1)].reshape(SEQ * SLOTS * 2, HD)
        old_s = SK[:, pl.ds(xat(k), 1)].reshape(2 * SINKS, HD)
        s = jnp.where(valid, nt(q, old) * scale, -1e30)
        s_s = jnp.where(valid_s, nt(q, old_s) * scale, -1e30)
        top = jnp.maximum(
            jnp.max(s, axis=-1, keepdims=True), jnp.max(s_s, axis=-1, keepdims=True)
        )
        w = jnp.where(valid, jnp.exp(s - top), 0.0)
        wt_s = jnp.where(valid_s, jnp.exp(s_s - top), 0.0)
        total = jnp.sum(w, axis=-1, keepdims=True) + jnp.sum(
            wt_s, axis=-1, keepdims=True
        )
        shifted = pltpu.roll(w, 1, 1).astype(jnp.bfloat16)
        shifted_s = nn(wt_s.astype(jnp.bfloat16), move).astype(jnp.bfloat16)
        weighted = nn(shifted, old) + nn(shifted_s, old_s)
        tree = reach > 0.5
        t = jnp.where(tree, nt(q, keys[k]) * scale, -1e30)
        joint = jnp.maximum(top, jnp.max(t, axis=-1, keepdims=True))
        tw = jnp.where(tree, jnp.exp(t - joint), 0.0)
        ratio = jnp.exp(top - joint)
        summed = nn(tw.astype(jnp.bfloat16), values[k])
        below = total * ratio + jnp.sum(tw, axis=-1, keepdims=True)
        done = ((weighted * ratio + summed) / below).astype(jnp.bfloat16)
        if k == 0:
            ATT[x] = done
        else:
            att[k - 1] = done
            for dx, dz in parts[turn]:
                hop_b(dx, dz)
            send(att.at[k - 1], ATT.at[x], a_s, a_r, idx(k, 0))

    for dx, dz in parts[3]:
        hop_b(dx, dz)
    for dz in (0, -1, 1, -2, 2, -3, 3, -4):
        hop_b(-2, dz)
    all_of(ATT.at[pl.ds(0, X - 1)], a_r)
    a = jnp.concatenate([ATT[h] for h in range(HEADS)], axis=1)
    all_of(WO.at[pl.ds(0, SEQ // CORES)], bsib_r)
    wide_group = SEQ // TP
    turns = (2, 1, 3, 0)
    for at, k in enumerate(turns):
        t = lax.rem(tp + k, TP)
        right = WO[pl.ds(t * wide_group, wide_group)].reshape(WIDTH, WIDTH)
        part[t] = nt(a, right).astype(jnp.bfloat16)
        if at:
            t = lax.rem(tp + turns[at - 1], TP)
            pltpu.make_async_remote_copy(
                src_ref=part.at[t], dst_ref=PG.at[tp], send_sem=ps, recv_sem=pr,
                device_id={"tp": t},
            ).start()

    others = pl.ds(0, SEQ - 1)
    pieces = SEQ // CORES
    all_of(N.at[pl.ds(0, X - 1)], t_s)
    all_of(WH.at[:, pl.ds(0, X - 1), 0], wx_s)
    all_of(WH.at[:, :, pl.ds(0, Z - 1)], w_s)
    all_of(WH.at[:, :, pl.ds(0, Z)], wsib_s)
    all_of(WO.at[pl.ds(0, pieces - 1)], b_s)
    all_of(WO.at[pl.ds(0, pieces)], bsib_s)
    all_of(packed.at[others], kv_s)
    all_of(att, a_s)

    @pl.when(me < SINKS)
    def _():
        all_of(sinks.at[others], sk_s)

    own_g.wait()
    all_of(G.at[others], gr)
    arrived[...] = G[...]
    all_of(PG.at[pl.ds(0, TP - 1)], pr)
    below = part[tp].astype(jnp.float32)
    for k in range(1, TP):
        below = below + PG[lax.rem(tp + k, TP)].astype(jnp.float32)
    gathered[...] = below.astype(jnp.bfloat16)
    all_of(part.at[pl.ds(0, TP - 1)], ps)
    all_of(fresh.at[others], gs)


def final_kernel(deal, code, G, gathered, cache, branch, new_cache, sem):
    copy = pltpu.make_async_copy(cache, new_cache, sem)
    copy.start()
    branch[...] = gathered[...]
    copy.wait()

    def place(i, carry):
        r = deal[i]
        spot = code[0, r]
        far, near = lax.shift_right_logical(i, 4), i & (COLUMN - 1)

        @pl.when(spot >= 0)
        def _():
            for h in range(HEADS):
                new_cache[r, spot, :, h * HD:(h + 1) * HD] = G[h * COLUMN + near, far]

        return carry

    lax.fori_loop(0, ROWS, place, 0, unroll=8)


def whole():
    return pl.BlockSpec(memory_space=pltpu.VMEM)


def shaped(shape, dtype=jnp.bfloat16):
    return jax.ShapeDtypeStruct(shape, dtype)


def run_whole(deal, lengths, leaves, tokens, parents, freq, spans, tips, cache, wq, wo):
    dma = pltpu.SemaphoreType.DMA
    vmem = pltpu.VMEM
    half = jnp.bfloat16
    return pl.pallas_call(
        whole_kernel,
        name="whole",
        in_specs=[pl.BlockSpec(memory_space=pltpu.SMEM)] * 3 + [whole()] * 8,
        out_specs=[whole()] * 3,
        out_shape=[
            shaped((ROWS, WIDTH)),
            shaped((SEQ, X, 2, HD)),
            shaped((1, ROWS), jnp.int32),
        ],
        scratch_shapes=[
            vmem((SEQ, X, 2 * SLOTS, HD), half),
            vmem((SEQ, X, 2, HD), half),
            vmem((X, ROWS, DEEP), half),
            vmem((3, X, COLUMN, DEEP // SEQ, HD), half),
            vmem((SEQ, DEEP // SEQ, WIDTH), half),
            vmem((SEQ, X, 2 * SLOTS, HD), half),
            vmem((SINKS, X, 2, HD), half),
            vmem((3, X * ROWS, HD), jnp.float32),
            vmem((X - 1, ROWS, HD), half),
            vmem((X, ROWS, HD), half),
            vmem((TP, ROWS, WIDTH), half),
            vmem((TP, ROWS, WIDTH), half),
            vmem((SEQ, X, 2, HD), half),
            vmem((SEQ, X, 2, HD), half),
            vmem((ROWS, HD), jnp.int32),
            dma((5,)), dma((4,)), dma((Z,)), dma((X, Z)),
        ] + [dma] * 19,
        compiler_params=pltpu.CompilerParams(collective_id=0, has_side_effects=True),
    )(deal, lengths, leaves, tokens, parents, freq, spans, tips, cache, wq, wo)


def run_final(deal, code, arrived, gathered, cache):
    return pl.pallas_call(
        final_kernel,
        name="final",
        grid_spec=pltpu.PrefetchScalarGridSpec(
            num_scalar_prefetch=2,
            in_specs=[whole(), whole(), pl.BlockSpec(memory_space=pl.ANY)],
            out_specs=[whole()] * 2,
            scratch_shapes=[pltpu.SemaphoreType.DMA],
        ),
        out_shape=[shaped((ROWS, WIDTH)), shaped(cache.shape)],
    )(deal, code, arrived, gathered, cache)


def on_device(tokens, qkv_weight, out_weight, kv_cache, lengths, parents, leaves, deal):
    cache = kv_cache.reshape(kv_cache.shape[0], kv_cache.shape[1], 2, WIDTH)
    half = np.arange(HD, dtype=np.float64) % (HD // 2)
    freq = jnp.asarray((10000.0 ** (-2.0 * half / HD)).astype(np.float32)[None, :])
    wq = jnp.transpose(qkv_weight, (1, 0, 2))
    wo = jnp.transpose(out_weight, (1, 0))
    gathered, arrived, code = run_whole(
        deal, lengths, leaves, tokens, parents, freq,
        lengths.reshape(1, ROWS), leaves.reshape(1, ROWS), cache, wq, wo,
    )
    branch, new_cache = run_final(deal, code, arrived, gathered, cache)
    return branch, new_cache.reshape(kv_cache.shape)


def solution(mesh):
    placed = (
        P("seq", None),
        P("seq", None, "tp"),
        P("tp", "seq"),
        P(None, None, "seq", None, "tp"),
        P(),
        P(),
        P(),
        P(),
    )
    return jax.shard_map(
        on_device,
        mesh=mesh,
        in_specs=placed,
        out_specs=(P("seq", "tp"), P(None, None, "seq", None, "tp")),
        check_vma=False,
    )
```

time: 72.8 us -> 70.7 us (0.971)
  Pallas kernels: 71.2 us -> 69.9 us
    pallas_call x1, Pallas kernels: 66.9 us -> 65.4 us  [run_whole(): pl.pallas_call(whole_kernel, name='whole', in_specs=[pl.BlockSpec(memory_...]
where the time goes in v4:
time: 70.7 us; the launch traced here: 70.5 us
  Pallas kernels  69.9 us (99%)
    pallas_call x1, Pallas kernels, run_whole(): pl.pallas_call(whole_kernel, name='whole', in_specs=[pl.BlockSpec(memory_...  65.4 us
    pallas_call x1, Pallas kernels, run_final(): pl.pallas_call(final_kernel, name='final', grid_spec=pltpu.PrefetchScalar...  4.51 us

profile of v4, /device:TPU:1, one launch (start us, length us, event | category | flops | bytes accessed | tf_op | source)
XLA Modules:
  0.0 70.5 jit_solution(2688916277182241017)
XLA Ops:
  0.6 65.4 %whole.1 = (bf16[64,512]{1,0:T(8,128)(2,1)}, bf16[64,4,2,128]{3,2,1,0:T(2,128)(2,1)}, s32[1,64]{1,0:T(1,128)}) custom-call(s32[64]{0:T(128)} %deal.3, s32[64]{0:T(128)} %lengths.1, s32[64]{0:T(128)} %leaves.1, bf16[64,2048]{1,0:T(8,128)(2,1)} %tokens.1, s32[64,64]{1,0:T(8,128)} %parents.1, f32[1,128]{1,0:T(1,128)} %constant.2.clone.freq, s32[1,64]{1,0:T(1,128)} %bitcast.12, ...), custom_call_target="tpu_custom_call" | custom-call | tf_op jit(solution)/shard_map/whole/pallas_call | solution.py:468
  66.0 4.5 %final.1 = (bf16[64,512]{1,0:T(8,128)(2,1)}, bf16[64,8,2,512]{3,2,1,0:T(2,128)(2,1)}) custom-call(s32[64]{0:T(128)} %deal.3, s32[1,64]{1,0:T(1,128)} %get-tuple-element.7.code, bf16[64,4,2,128]{3,2,1,0:T(2,128)(2,1)} %get-tuple-element.8.G, bf16[64,512]{1,0:T(8,128)(2,1)} %get-tuple-element.9.gathered, bf16[64,8,2,512]{3,2,1,0:T(2,128)(2,1)} %bitcast.9), custom_call_target="tpu_custom_call" | custom-call | tf_op jit(solution)/shard_map/final/pallas_call | solution.py:501

commit v5 on v4

--- a/solution.py
+++ b/solution.py
@@ -109,10 +109,58 @@
 
     pl.semaphore_wait(barrier, SEQ + TP - 2)
 
+    def send_w(dz, step):
+        at = WH.at[:, :, qat(dz)]
+        if step == 0:
+            send(at, at, wsib_s, wsib_r, me + 1 - 2 * c)
+        else:
+            send(at, at, w_s, wr.at[(dz - step) % Z], idx(0, step))
+
+    def hop_w(dz):
+        at = WH.at[:, :, qat(dz)]
+        all_of(at, wr.at[dz % Z])
+        if -4 < dz < 0:
+            send_w(dz, 1)
+        elif 0 < dz < 3:
+            send_w(dz, -1)
+        send_w(dz, 0)
+
+    def send_b(dx, dz, way):
+        at = idx(dx, dz)
+        src = wo if (dx, dz) == (0, 0) else WO.at[at]
+        if way == "s":
+            send(src, WO.at[at], bsib_s, bsib_r, me + 1 - 2 * c)
+        else:
+            ox, oz = {"x+": (1, 0), "x-": (-1, 0), "z+": (0, 1), "z-": (0, -1)}[way]
+            send(
+                src, WO.at[at], b_s, br.at[(dx - ox) % X, (dz - oz) % Z], idx(ox, oz)
+            )
+
+    def hop_b(dx, dz):
+        if (dx, dz) != (0, 0):
+            all_of(WO.at[idx(dx, dz)], br.at[dx % X, dz % Z])
+        out = []
+        if dx == 0:
+            if dz == 0:
+                out += ["z+", "z-"]
+            elif -4 < dz < 0:
+                out += ["z+"]
+            elif 0 < dz < 3:
+                out += ["z-"]
+            out += ["x+", "x-"]
+        elif dx == -1 and dz % 2 == 0:
+            out += ["x+"]
+        elif dx == 1 and dz % 2 == 1:
+            out += ["x-"]
+        for way in out + ["s"]:
+            send_b(dx, dz, way)
+
     for k in (2, 1, 3):
         send(
             wq.at[:, :, side(xat(k))], WH.at[:, x, column], wx_s, wx_r, idx(k, 0)
         )
+    own_b.wait()
+    hop_b(0, 0)
     send(N.at[x], N.at[x], t_s, tr.at[0], idx(1, 0))
     send(N.at[x], N.at[x], t_s, tr.at[1], idx(-1, 0))
 
@@ -176,52 +224,6 @@
             jnp.where(sub == lane, code, 0), axis=0, keepdims=True
         )
 
-    def send_w(dz, step):
-        at = WH.at[:, :, qat(dz)]
-        if step == 0:
-            send(at, at, wsib_s, wsib_r, me + 1 - 2 * c)
-        else:
-            send(at, at, w_s, wr.at[(dz - step) % Z], idx(0, step))
-
-    def hop_w(dz):
-        at = WH.at[:, :, qat(dz)]
-        all_of(at, wr.at[dz % Z])
-        if -4 < dz < 0:
-            send_w(dz, 1)
-        elif 0 < dz < 3:
-            send_w(dz, -1)
-        send_w(dz, 0)
-
-    def send_b(dx, dz, way):
-        at = idx(dx, dz)
-        src = wo if (dx, dz) == (0, 0) else WO.at[at]
-        if way == "s":
-            send(src, WO.at[at], bsib_s, bsib_r, me + 1 - 2 * c)
-        else:
-            ox, oz = {"x+": (1, 0), "x-": (-1, 0), "z+": (0, 1), "z-": (0, -1)}[way]
-            send(
-                src, WO.at[at], b_s, br.at[(dx - ox) % X, (dz - oz) % Z], idx(ox, oz)
-            )
-
-    def hop_b(dx, dz):
-        if (dx, dz) != (0, 0):
-            all_of(WO.at[idx(dx, dz)], br.at[dx % X, dz % Z])
-        out = []
-        if dx == 0:
-            if dz == 0:
-                out += ["z+", "z-"]
-            elif -4 < dz < 0:
-                out += ["z+"]
-            elif 0 < dz < 3:
-                out += ["z-"]
-            out += ["x+", "x-"]
-        elif dx == -1 and dz % 2 == 0:
-            out += ["x+"]
-        elif dx == 1 and dz % 2 == 1:
-            out += ["x-"]
-        for way in out + ["s"]:
-            send_b(dx, dz, way)
-
     order = (2, 1, 3, 0)
     told = {order[0]: describe(order[0])}
 
@@ -230,19 +232,22 @@
     send_w(0, 1)
     send_w(0, -1)
     send_w(0, 0)
+    hop_b(0, -1)
+    hop_b(0, 1)
     scatter(*KV_PARTS[1])
     told[order[1]] = describe(order[1])
 
     left, right = pl.ds(0, DEEP // 2), pl.ds(DEEP // 2, DEEP // 2)
+    hop_w(-1)
+    hop_w(1)
+    hop_b(0, -2)
+    hop_b(0, 2)
     all_of(N.at[0], tr.at[0])
     at = N.at[xat(-1), :, left]
     send(at, at, t_s, tr.at[2], idx(1, 0))
     all_of(N.at[0], tr.at[1])
     at = N.at[xat(1), :, right]
     send(at, at, t_s, tr.at[3], idx(-1, 0))
-
-    hop_w(-1)
-    hop_w(1)
     scatter(*KV_PARTS[2])
 
     @pl.when(me < SINKS)
@@ -259,20 +264,27 @@
     told[order[2]] = describe(order[2])
     hop_w(-2)
     hop_w(2)
+    hop_b(0, -3)
+    hop_b(0, 3)
     scatter(*KV_PARTS[3])
     told[order[3]] = describe(order[3])
+    hop_b(-1, 0)
+    hop_b(1, 0)
     hop_w(-3)
     hop_w(3)
+    hop_b(0, -4)
     scatter(*KV_PARTS[4])
-    own_b.wait()
-    hop_b(0, 0)
     table()
+    for dz in (-1, 1):
+        hop_b(-1, dz)
+        hop_b(1, dz)
     hop_w(-4)
+    for dz in (-2, 2):
+        hop_b(-1, dz)
+        hop_b(1, dz)
 
     all_of(N.at[0, :, left], tr.at[2])
     all_of(N.at[0, :, right], tr.at[3])
-    hop_b(0, -1)
-    hop_b(0, 1)
     all_of(WH.at[:, :, pl.ds(0, Z)], wsib_r)
     deep = COLUMN * (DEEP // SEQ)
     rows_all = X * ROWS
@@ -283,9 +295,6 @@
             term = nn(mine, WH[kind, block].reshape(deep, HD))
             total = term if total is None else total + term
         acc[kind] = total
-        if kind == 0:
-            hop_b(0, -2)
-            hop_b(0, 2)
 
     twice = lax.broadcasted_iota(jnp.int32, (2 * SEQ, SEQ), 0)
     once = lax.broadcasted_iota(jnp.int32, (2 * SEQ, SEQ), 1)
@@ -306,8 +315,9 @@
         pick_v = nn(odd, pick).astype(jnp.bfloat16)
         mixed = (nn(pick_k, keys[k]) + nn(pick_v, values[k])).astype(jnp.bfloat16)
         fresh[:, xat(k)] = mixed.reshape(SEQ, 2, HD)
-    hop_b(0, -3)
-    hop_b(0, 3)
+    for dz in (-3, 3, -4):
+        hop_b(-1, dz)
+        hop_b(1, dz)
 
     own_g = pltpu.make_async_copy(fresh.at[me], G.at[me], own_sem.at[4])
     own_g.start()
@@ -319,9 +329,8 @@
 
     lax.fori_loop(1, SEQ, hand, 0)
 
-    later = [(dx, dz) for dz in (0, -1, 1, -2, 2, -3, 3, -4) for dx in (-1, 1)]
-    later.insert(8, (0, -4))
-    parts = [later[0:4], later[4:9], later[9:13], later[13:17]]
+    later = [(-2, dz) for dz in (0, -1, 1, -2, 2, -3, 3, -4)]
+    parts = [later[0:3], later[3:5], later[5:7], later[7:8]]
 
     own_kv.wait()
     all_of(KV.at[pl.ds(0, SEQ - 1)], kv_r)
@@ -387,8 +396,6 @@
 
     for dx, dz in parts[3]:
         hop_b(dx, dz)
-    for dz in (0, -1, 1, -2, 2, -3, 3, -4):
-        hop_b(-2, dz)
     all_of(ATT.at[pl.ds(0, X - 1)], a_r)
     a = jnp.concatenate([ATT[h] for h in range(HEADS)], axis=1)
     all_of(WO.at[pl.ds(0, SEQ // CORES)], bsib_r)

time: 70.7 us -> 58.8 us (0.83)
  the two profiles are of different devices: /device:TPU:1 before, /device:TPU:37 now
where the time goes in v5:
time: 58.8 us; the launch traced here: 58.6 us
  Pallas kernels  58 us (99%)
  between operations  0.64 us (1%)
    pallas_call x1, Pallas kernels, run_whole(): pl.pallas_call(whole_kernel, name='whole', in_specs=[pl.BlockSpec(memory_...  53.5 us
    pallas_call x1, Pallas kernels, run_final(): pl.pallas_call(final_kernel, name='final', grid_spec=pltpu.PrefetchScalar...  4.48 us

profile of v5, /device:TPU:37, one launch (start us, length us, event | category | flops | bytes accessed | tf_op | source)
XLA Modules:
  0.0 58.6 jit_solution(6983108303970470907)
XLA Ops:
  0.6 53.5 %whole.1 = (bf16[64,512]{1,0:T(8,128)(2,1)}, bf16[64,4,2,128]{3,2,1,0:T(2,128)(2,1)}, s32[1,64]{1,0:T(1,128)}) custom-call(s32[64]{0:T(128)} %deal.3, s32[64]{0:T(128)} %lengths.1, s32[64]{0:T(128)} %leaves.1, bf16[64,2048]{1,0:T(8,128)(2,1)} %tokens.1, s32[64,64]{1,0:T(8,128)} %parents.1, f32[1,128]{1,0:T(1,128)} %constant.2.clone.freq, s32[1,64]{1,0:T(1,128)} %bitcast.12, ...), custom_call_target="tpu_custom_call" | custom-call | tf_op jit(solution)/shard_map/whole/pallas_call | solution.py:475
  54.1 4.5 %final.1 = (bf16[64,512]{1,0:T(8,128)(2,1)}, bf16[64,8,2,512]{3,2,1,0:T(2,128)(2,1)}) custom-call(s32[64]{0:T(128)} %deal.3, s32[1,64]{1,0:T(1,128)} %get-tuple-element.7.code, bf16[64,4,2,128]{3,2,1,0:T(2,128)(2,1)} %get-tuple-element.8.G, bf16[64,512]{1,0:T(8,128)(2,1)} %get-tuple-element.9.gathered, bf16[64,8,2,512]{3,2,1,0:T(2,128)(2,1)} %bitcast.9), custom_call_target="tpu_custom_call" | custom-call | tf_op jit(solution)/shard_map/final/pallas_call | solution.py:508

commit v6 on v5

--- a/solution.py
+++ b/solution.py
@@ -39,7 +39,7 @@
     deal, lengths, leaves, tokens, parents, freq, spans, tips, cache, wq, wo,
     gathered, arrived, code_out,
     packed, sinks, N, WH, WO, KV, SK, acc, att, ATT, part, PG, fresh, G, par_pad,
-    own_sem, tr, wr, br,
+    own_sem, tr, wr, br, gate,
     t_s, wx_s, wx_r, w_s, wsib_s, wsib_r, b_s, bsib_s, bsib_r,
     kv_s, kv_r, sk_s, sk_r, a_s, a_r, ps, pr, gs, gr,
 ):
@@ -73,11 +73,13 @@
 
     barrier = pltpu.get_barrier_semaphore()
 
-    def greet(k, carry):
-        pl.semaphore_signal(barrier, 1, device_id={"seq": lax.rem(me + k, SEQ)})
-        return carry
-
-    lax.fori_loop(1, SEQ, greet, 0)
+    def mate(k):
+        return x * COLUMN + lax.rem(column + k, COLUMN)
+
+    for k in range(1, COLUMN):
+        pl.semaphore_signal(barrier, 1, device_id={"seq": mate(k)})
+    for k in range(1, X):
+        pl.semaphore_signal(barrier, 1, device_id={"seq": xat(k) * COLUMN + column})
     for k in range(1, TP):
         pl.semaphore_signal(barrier, 1, device_id={"tp": lax.rem(tp + k, TP)})
 
@@ -107,7 +109,9 @@
 
     lax.fori_loop(0, ROWS, pack, 0)
 
-    pl.semaphore_wait(barrier, SEQ + TP - 2)
+    pl.semaphore_wait(barrier, COLUMN + X + TP - 3)
+    for k in range(1, COLUMN):
+        pl.semaphore_signal(gate, 1, device_id={"seq": mate(k)})
 
     def send_w(dz, step):
         at = WH.at[:, :, qat(dz)]
@@ -143,9 +147,9 @@
         if dx == 0:
             if dz == 0:
                 out += ["z+", "z-"]
-            elif -4 < dz < 0:
+            elif -3 < dz < 0:
                 out += ["z+"]
-            elif 0 < dz < 3:
+            elif 0 < dz < 4:
                 out += ["z-"]
             out += ["x+", "x-"]
         elif dx == -1 and dz % 2 == 0:
@@ -169,13 +173,14 @@
 
     def scatter(low, high):
         def one(k, carry):
-            t = lax.rem(me + k, SEQ)
+            t = xat(k // COLUMN) * COLUMN + lax.rem(column + k, COLUMN)
             send(packed.at[t], KV.at[me], kv_s, kv_r, t)
             return carry
 
         lax.fori_loop(low, high, one, 0)
 
     scatter(*KV_PARTS[0])
+    pl.semaphore_wait(gate, COLUMN - 1)
 
     sub = lax.broadcasted_iota(jnp.int32, (ROWS, ROWS), 0)
     lane = lax.broadcasted_iota(jnp.int32, (ROWS, ROWS), 1)
@@ -499,6 +504,7 @@
             vmem((SEQ, X, 2, HD), half),
             vmem((ROWS, HD), jnp.int32),
             dma((5,)), dma((4,)), dma((Z,)), dma((X, Z)),
+            pltpu.SemaphoreType.REGULAR,
         ] + [dma] * 19,
         compiler_params=pltpu.CompilerParams(collective_id=0, has_side_effects=True),
     )(deal, lengths, leaves, tokens, parents, freq, spans, tips, cache, wq, wo)

time: 58.8 us -> 57.2 us (0.973)
  the two profiles are of different devices: /device:TPU:37 before, /device:TPU:1 now
where the time goes in v6:
time: 57.2 us; the launch traced here: 57 us
  Pallas kernels  56.4 us (99%)
  between operations  0.64 us (1%)
    pallas_call x1, Pallas kernels, run_whole(): pl.pallas_call(whole_kernel, name='whole', in_specs=[pl.BlockSpec(memory_...  51.8 us
    pallas_call x1, Pallas kernels, run_final(): pl.pallas_call(final_kernel, name='final', grid_spec=pltpu.PrefetchScalar...  4.58 us

profile of v6, /device:TPU:1, one launch (start us, length us, event | category | flops | bytes accessed | tf_op | source)
XLA Modules:
  0.0 57.0 jit_solution(17382419772503619973)
XLA Ops:
  0.6 51.8 %whole.1 = (bf16[64,512]{1,0:T(8,128)(2,1)}, bf16[64,4,2,128]{3,2,1,0:T(2,128)(2,1)}, s32[1,64]{1,0:T(1,128)}) custom-call(s32[64]{0:T(128)} %deal.3, s32[64]{0:T(128)} %lengths.1, s32[64]{0:T(128)} %leaves.1, bf16[64,2048]{1,0:T(8,128)(2,1)} %tokens.1, s32[64,64]{1,0:T(8,128)} %parents.1, f32[1,128]{1,0:T(1,128)} %constant.2.clone.freq, s32[1,64]{1,0:T(1,128)} %bitcast.12, ...), custom_call_target="tpu_custom_call" | custom-call | tf_op jit(solution)/shard_map/whole/pallas_call | solution.py:480
  52.5 4.6 %final.1 = (bf16[64,512]{1,0:T(8,128)(2,1)}, bf16[64,8,2,512]{3,2,1,0:T(2,128)(2,1)}) custom-call(s32[64]{0:T(128)} %deal.3, s32[1,64]{1,0:T(1,128)} %get-tuple-element.7.code, bf16[64,4,2,128]{3,2,1,0:T(2,128)(2,1)} %get-tuple-element.8.G, bf16[64,512]{1,0:T(8,128)(2,1)} %get-tuple-element.9.gathered, bf16[64,8,2,512]{3,2,1,0:T(2,128)(2,1)} %bitcast.9), custom_call_target="tpu_custom_call" | custom-call | tf_op jit(solution)/shard_map/final/pallas_call | solution.py:514

commit v7 on v6

--- a/solution.py
+++ b/solution.py
@@ -15,6 +15,8 @@
 TP = 4
 COLUMN = Z * CORES
 ROWS = 64
+CPOS = 8
+CHUNKS = 4
 SLOTS = 4
 WIDTH = 512
 HEADS = WIDTH // HD
@@ -36,9 +38,9 @@
 
 
 def whole_kernel(
-    deal, lengths, leaves, tokens, parents, freq, spans, tips, cache, wq, wo,
+    deal, lengths, leaves, tokens, parents, freq, spans, tips, deals, cache, wq, wo,
     gathered, arrived, code_out,
-    packed, sinks, N, WH, WO, KV, SK, acc, att, ATT, part, PG, fresh, G, par_pad,
+    packed, sinks, N, WH, WO, KV, SK, acc, att, ATT, part, PG, fresh, G, par_pad, held,
     own_sem, tr, wr, br, gate,
     t_s, wx_s, wx_r, w_s, wsib_s, wsib_r, b_s, bsib_s, bsib_r,
     kv_s, kv_r, sk_s, sk_r, a_s, a_r, ps, pr, gs, gr,
@@ -71,6 +73,8 @@
             device_id={"seq": target},
         ).start()
 
+    own_cache = pltpu.make_async_copy(cache, held, own_sem.at[3])
+    own_cache.start()
     barrier = pltpu.get_barrier_semaphore()
 
     def mate(k):
@@ -99,14 +103,15 @@
         r = deal[t]
         base = jnp.maximum(lengths[r] - WINDOW, 0)
         first = lax.shift_right_logical(base - me + (SEQ - 1), 6)
-        rows = cache[r, pl.ds(first, SLOTS)].reshape(2 * SLOTS, WIDTH)
-        sunk = cache[r, 0]
+        rows = held[r, pl.ds(first, SLOTS)].reshape(2 * SLOTS, WIDTH)
+        sunk = held[r, 0]
         far, near = t // COLUMN, lax.rem(t, COLUMN)
         for h in range(HEADS):
             packed[h * COLUMN + near, far] = rows[:, h * HD:(h + 1) * HD]
             sinks[h * COLUMN + near, far] = sunk[:, h * HD:(h + 1) * HD]
         return carry
 
+    own_cache.wait()
     lax.fori_loop(0, ROWS, pack, 0)
 
     pl.semaphore_wait(barrier, COLUMN + X + TP - 3)
@@ -221,9 +226,10 @@
         tip = jnp.sum(jnp.where(sub == lane, tips[...], 0), axis=1, keepdims=True)
         span = jnp.sum(jnp.where(sub == lane, spans[...], 0), axis=1, keepdims=True)
         end = jnp.sum(jnp.where(lanes == tip, climb, 0), axis=1, keepdims=True)
+        tree_of = jnp.sum(jnp.where(deals[...] == sub, lane, 0), axis=1, keepdims=True)
         ahead = (me - span + 8 * SEQ) & (SEQ - 1)
         code = jnp.where(
-            ahead <= end, lax.shift_right_logical(span + ahead, 6), -1
+            ahead <= end, lax.shift_right_logical(span + ahead, 6) + CPOS * tree_of, -1
         )
         code_out[...] = jnp.sum(
             jnp.where(sub == lane, code, 0), axis=0, keepdims=True
@@ -444,25 +450,36 @@
     all_of(fresh.at[others], gs)
 
 
-def final_kernel(deal, code, G, gathered, cache, branch, new_cache, sem):
-    copy = pltpu.make_async_copy(cache, new_cache, sem)
-    copy.start()
+def final_kernel(code, G, gathered, cache, branch, new_cache, held, come, leave):
+    chunk = ROWS // CHUNKS
+    spans = [pl.ds(j * chunk, chunk) for j in range(CHUNKS)]
+    ins = [
+        pltpu.make_async_copy(cache.at[at], held.at[at], come.at[j])
+        for j, at in enumerate(spans)
+    ]
+    outs = [
+        pltpu.make_async_copy(held.at[at], new_cache.at[at], leave.at[j])
+        for j, at in enumerate(spans)
+    ]
+    for copy in ins:
+        copy.start()
     branch[...] = gathered[...]
-    copy.wait()
-
-    def place(i, carry):
-        r = deal[i]
-        spot = code[0, r]
-        far, near = lax.shift_right_logical(i, 4), i & (COLUMN - 1)
-
-        @pl.when(spot >= 0)
-        def _():
-            for h in range(HEADS):
-                new_cache[r, spot, :, h * HD:(h + 1) * HD] = G[h * COLUMN + near, far]
-
-        return carry
-
-    lax.fori_loop(0, ROWS, place, 0, unroll=8)
+    for j in range(CHUNKS):
+        ins[j].wait()
+        for r in range(j * chunk, (j + 1) * chunk):
+            tag = code[0, r]
+
+            @pl.when(tag >= 0)
+            def _():
+                spot = tag & (CPOS - 1)
+                near = lax.shift_right_logical(tag, 3) & (COLUMN - 1)
+                far = lax.shift_right_logical(tag, 7)
+                for h in range(HEADS):
+                    held[r, spot, :, h * HD:(h + 1) * HD] = G[h * COLUMN + near, far]
+
+        outs[j].start()
+    for copy in outs:
+        copy.wait()
 
 
 def whole():
@@ -473,14 +490,15 @@
     return jax.ShapeDtypeStruct(shape, dtype)
 
 
-def run_whole(deal, lengths, leaves, tokens, parents, freq, spans, tips, cache, wq, wo):
+def run_whole(deal, lengths, leaves, tokens, parents, freq, spans, tips, deals, cache, wq, wo):
     dma = pltpu.SemaphoreType.DMA
     vmem = pltpu.VMEM
     half = jnp.bfloat16
     return pl.pallas_call(
         whole_kernel,
         name="whole",
-        in_specs=[pl.BlockSpec(memory_space=pltpu.SMEM)] * 3 + [whole()] * 8,
+        in_specs=[pl.BlockSpec(memory_space=pltpu.SMEM)] * 3 + [whole()] * 6
+        + [pl.BlockSpec(memory_space=pl.ANY)] + [whole()] * 2,
         out_specs=[whole()] * 3,
         out_shape=[
             shaped((ROWS, WIDTH)),
@@ -503,25 +521,27 @@
             vmem((SEQ, X, 2, HD), half),
             vmem((SEQ, X, 2, HD), half),
             vmem((ROWS, HD), jnp.int32),
+            vmem(cache.shape, half),
             dma((5,)), dma((4,)), dma((Z,)), dma((X, Z)),
             pltpu.SemaphoreType.REGULAR,
         ] + [dma] * 19,
         compiler_params=pltpu.CompilerParams(collective_id=0, has_side_effects=True),
-    )(deal, lengths, leaves, tokens, parents, freq, spans, tips, cache, wq, wo)
-
-
-def run_final(deal, code, arrived, gathered, cache):
+    )(deal, lengths, leaves, tokens, parents, freq, spans, tips, deals, cache, wq, wo)
+
+
+def run_final(code, arrived, gathered, cache):
+    dma = pltpu.SemaphoreType.DMA
+    outside = pl.BlockSpec(memory_space=pl.ANY)
     return pl.pallas_call(
         final_kernel,
         name="final",
-        grid_spec=pltpu.PrefetchScalarGridSpec(
-            num_scalar_prefetch=2,
-            in_specs=[whole(), whole(), pl.BlockSpec(memory_space=pl.ANY)],
-            out_specs=[whole()] * 2,
-            scratch_shapes=[pltpu.SemaphoreType.DMA],
-        ),
+        in_specs=[pl.BlockSpec(memory_space=pltpu.SMEM), whole(), whole(), outside],
+        out_specs=[whole(), outside],
         out_shape=[shaped((ROWS, WIDTH)), shaped(cache.shape)],
-    )(deal, code, arrived, gathered, cache)
+        scratch_shapes=[
+            pltpu.VMEM(cache.shape, jnp.bfloat16), dma((CHUNKS,)), dma((CHUNKS,)),
+        ],
+    )(code, arrived, gathered, cache)
 
 
 def on_device(tokens, qkv_weight, out_weight, kv_cache, lengths, parents, leaves, deal):
@@ -532,9 +552,10 @@
     wo = jnp.transpose(out_weight, (1, 0))
     gathered, arrived, code = run_whole(
         deal, lengths, leaves, tokens, parents, freq,
-        lengths.reshape(1, ROWS), leaves.reshape(1, ROWS), cache, wq, wo,
+        lengths.reshape(1, ROWS), leaves.reshape(1, ROWS), deal.reshape(1, ROWS),
+        cache, wq, wo,
     )
-    branch, new_cache = run_final(deal, code, arrived, gathered, cache)
+    branch, new_cache = run_final(code, arrived, gathered, cache)
     return branch, new_cache.reshape(kv_cache.shape)
 
 

time: 57.2 us -> 56.2 us (0.983)
  Pallas kernels: 56.4 us -> 55.4 us
    pallas_call x1, Pallas kernels: 4.58 us -> 3.79 us  [run_final(): pl.pallas_call(final_kernel, name='final', in_specs=[pl.BlockSpec(memory_...]
where the time goes in v7:
time: 56.2 us; the launch traced here: 56 us
  Pallas kernels  55.4 us (99%)
  between operations  0.64 us (1%)
    pallas_call x1, Pallas kernels, run_whole(): pl.pallas_call(whole_kernel, name='whole', in_specs=[pl.BlockSpec(memory_...  51.6 us
    pallas_call x1, Pallas kernels, run_final(): pl.pallas_call(final_kernel, name='final', in_specs=[pl.BlockSpec(memory_...  3.79 us

profile of v7, /device:TPU:1, one launch (start us, length us, event | category | flops | bytes accessed | tf_op | source)
XLA Modules:
  0.0 56.0 jit_solution(18443579756898568284)
XLA Ops:
  0.6 51.6 %whole.1 = (bf16[64,512]{1,0:T(8,128)(2,1)}, bf16[64,4,2,128]{3,2,1,0:T(2,128)(2,1)}, s32[1,64]{1,0:T(1,128)}) custom-call(s32[64]{0:T(128)} %deal.1, s32[64]{0:T(128)} %lengths.1, s32[64]{0:T(128)} %leaves.1, bf16[64,2048]{1,0:T(8,128)(2,1)} %tokens.1, s32[64,64]{1,0:T(8,128)} %parents.1, f32[1,128]{1,0:T(1,128)} %constant.2.clone.freq, s32[1,64]{1,0:T(1,128)} %bitcast.14, ...), custom_call_target="tpu_custom_call" | custom-call | tf_op jit(solution)/shard_map/whole/pallas_call | solution.py:497
  52.2 3.8 %final.1 = (bf16[64,512]{1,0:T(8,128)(2,1)}, bf16[64,8,2,512]{3,2,1,0:T(2,128)(2,1)}) custom-call(s32[1,64]{1,0:T(1,128)} %get-tuple-element.7.code, bf16[64,4,2,128]{3,2,1,0:T(2,128)(2,1)} %get-tuple-element.8.G, bf16[64,512]{1,0:T(8,128)(2,1)} %get-tuple-element.9.gathered, bf16[64,8,2,512]{3,2,1,0:T(2,128)(2,1)} %bitcast.10), custom_call_target="tpu_custom_call" | custom-call | tf_op jit(solution)/shard_map/final/pallas_call | solution.py:535

commit v8 on v7

--- a/solution.py
+++ b/solution.py
@@ -118,21 +118,25 @@
     for k in range(1, COLUMN):
         pl.semaphore_signal(gate, 1, device_id={"seq": mate(k)})
 
-    def send_w(dz, step):
+    def half_w(dz, half):
+        return WH.at[:, pl.ds(half * (X // 2), X // 2), qat(dz)]
+
+    def send_w(dz, step, half):
+        at = half_w(dz, half)
+        send(at, at, w_s, wr.at[(dz - step) % Z, half], idx(0, step))
+
+    def pass_w(dz):
         at = WH.at[:, :, qat(dz)]
-        if step == 0:
-            send(at, at, wsib_s, wsib_r, me + 1 - 2 * c)
-        else:
-            send(at, at, w_s, wr.at[(dz - step) % Z], idx(0, step))
+        send(at, at, wsib_s, wsib_r, me + 1 - 2 * c)
 
     def hop_w(dz):
-        at = WH.at[:, :, qat(dz)]
-        all_of(at, wr.at[dz % Z])
-        if -4 < dz < 0:
-            send_w(dz, 1)
-        elif 0 < dz < 3:
-            send_w(dz, -1)
-        send_w(dz, 0)
+        for half in range(2):
+            all_of(half_w(dz, half), wr.at[dz % Z, half])
+            if -4 < dz < 0:
+                send_w(dz, 1, half)
+            elif 0 < dz < 3:
+                send_w(dz, -1, half)
+        pass_w(dz)
 
     def send_b(dx, dz, way):
         at = idx(dx, dz)
@@ -240,9 +244,10 @@
 
     own_w.wait()
     all_of(WH.at[:, pl.ds(0, X - 1), 0], wx_r)
-    send_w(0, 1)
-    send_w(0, -1)
-    send_w(0, 0)
+    for half in range(2):
+        send_w(0, 1, half)
+        send_w(0, -1, half)
+    pass_w(0)
     hop_b(0, -1)
     hop_b(0, 1)
     scatter(*KV_PARTS[1])
@@ -522,7 +527,7 @@
             vmem((SEQ, X, 2, HD), half),
             vmem((ROWS, HD), jnp.int32),
             vmem(cache.shape, half),
-            dma((5,)), dma((4,)), dma((Z,)), dma((X, Z)),
+            dma((5,)), dma((4,)), dma((Z, 2)), dma((X, Z)),
             pltpu.SemaphoreType.REGULAR,
         ] + [dma] * 19,
         compiler_params=pltpu.CompilerParams(collective_id=0, has_side_effects=True),

time: 56.2 us -> 55 us (0.979)
  Pallas kernels: 55.4 us -> 54.2 us
    pallas_call x1, Pallas kernels: 51.6 us -> 50.5 us  [run_whole(): pl.pallas_call(whole_kernel, name='whole', in_specs=[pl.BlockSpec(memory_...]
where the time goes in v8:
time: 55 us; the launch traced here: 54.8 us
  Pallas kernels  54.2 us (99%)
  between operations  0.64 us (1%)
    pallas_call x1, Pallas kernels, run_whole(): pl.pallas_call(whole_kernel, name='whole', in_specs=[pl.BlockSpec(memory_...  50.5 us
    pallas_call x1, Pallas kernels, run_final(): pl.pallas_call(final_kernel, name='final', in_specs=[pl.BlockSpec(memory_...  3.71 us

profile of v8, /device:TPU:1, one launch (start us, length us, event | category | flops | bytes accessed | tf_op | source)
XLA Modules:
  0.0 54.8 jit_solution(14065605527099153971)
XLA Ops:
  0.6 50.5 %whole.1 = (bf16[64,512]{1,0:T(8,128)(2,1)}, bf16[64,4,2,128]{3,2,1,0:T(2,128)(2,1)}, s32[1,64]{1,0:T(1,128)}) custom-call(s32[64]{0:T(128)} %deal.1, s32[64]{0:T(128)} %lengths.1, s32[64]{0:T(128)} %leaves.1, bf16[64,2048]{1,0:T(8,128)(2,1)} %tokens.1, s32[64,64]{1,0:T(8,128)} %parents.1, f32[1,128]{1,0:T(1,128)} %constant.2.clone.freq, s32[1,64]{1,0:T(1,128)} %bitcast.14, ...), custom_call_target="tpu_custom_call" | custom-call | tf_op jit(solution)/shard_map/whole/pallas_call | solution.py:502
  51.1 3.7 %final.1 = (bf16[64,512]{1,0:T(8,128)(2,1)}, bf16[64,8,2,512]{3,2,1,0:T(2,128)(2,1)}) custom-call(s32[1,64]{1,0:T(1,128)} %get-tuple-element.7.code, bf16[64,4,2,128]{3,2,1,0:T(2,128)(2,1)} %get-tuple-element.8.G, bf16[64,512]{1,0:T(8,128)(2,1)} %get-tuple-element.9.gathered, bf16[64,8,2,512]{3,2,1,0:T(2,128)(2,1)} %bitcast.10), custom_call_target="tpu_custom_call" | custom-call | tf_op jit(solution)/shard_map/final/pallas_call | solution.py:540

commit v9 on v8

--- a/solution.py
+++ b/solution.py
@@ -254,16 +254,16 @@
     told[order[1]] = describe(order[1])
 
     left, right = pl.ds(0, DEEP // 2), pl.ds(DEEP // 2, DEEP // 2)
-    hop_w(-1)
-    hop_w(1)
-    hop_b(0, -2)
-    hop_b(0, 2)
     all_of(N.at[0], tr.at[0])
     at = N.at[xat(-1), :, left]
     send(at, at, t_s, tr.at[2], idx(1, 0))
     all_of(N.at[0], tr.at[1])
     at = N.at[xat(1), :, right]
     send(at, at, t_s, tr.at[3], idx(-1, 0))
+    hop_w(-1)
+    hop_w(1)
+    hop_b(0, -2)
+    hop_b(0, 2)
     scatter(*KV_PARTS[2])
 
     @pl.when(me < SINKS)

time: 55 us -> 56.5 us (1.027)
  Pallas kernels: 54.2 us -> 55.7 us
    pallas_call x1, Pallas kernels: 50.5 us -> 51.9 us  [run_whole(): pl.pallas_call(whole_kernel, name='whole', in_specs=[pl.BlockSpec(memory_...]
where the time goes in v9:
time: 56.5 us; the launch traced here: 56.3 us
  Pallas kernels  55.7 us (99%)
  between operations  0.64 us (1%)
    pallas_call x1, Pallas kernels, run_whole(): pl.pallas_call(whole_kernel, name='whole', in_specs=[pl.BlockSpec(memory_...  51.9 us
    pallas_call x1, Pallas kernels, run_final(): pl.pallas_call(final_kernel, name='final', in_specs=[pl.BlockSpec(memory_...  3.79 us

profile of v9, /device:TPU:1, one launch (start us, length us, event | category | flops | bytes accessed | tf_op | source)
XLA Modules:
  0.0 56.3 jit_solution(16176937328604012013)
XLA Ops:
  0.6 51.9 %whole.1 = (bf16[64,512]{1,0:T(8,128)(2,1)}, bf16[64,4,2,128]{3,2,1,0:T(2,128)(2,1)}, s32[1,64]{1,0:T(1,128)}) custom-call(s32[64]{0:T(128)} %deal.1, s32[64]{0:T(128)} %lengths.1, s32[64]{0:T(128)} %leaves.1, bf16[64,2048]{1,0:T(8,128)(2,1)} %tokens.1, s32[64,64]{1,0:T(8,128)} %parents.1, f32[1,128]{1,0:T(1,128)} %constant.2.clone.freq, s32[1,64]{1,0:T(1,128)} %bitcast.14, ...), custom_call_target="tpu_custom_call" | custom-call | tf_op jit(solution)/shard_map/whole/pallas_call | solution.py:502
  52.6 3.8 %final.1 = (bf16[64,512]{1,0:T(8,128)(2,1)}, bf16[64,8,2,512]{3,2,1,0:T(2,128)(2,1)}) custom-call(s32[1,64]{1,0:T(1,128)} %get-tuple-element.7.code, bf16[64,4,2,128]{3,2,1,0:T(2,128)(2,1)} %get-tuple-element.8.G, bf16[64,512]{1,0:T(8,128)(2,1)} %get-tuple-element.9.gathered, bf16[64,8,2,512]{3,2,1,0:T(2,128)(2,1)} %bitcast.10), custom_call_target="tpu_custom_call" | custom-call | tf_op jit(solution)/shard_map/final/pallas_call | solution.py:540
